TPU v7x, 512 devices: a whole 4x4x16 slice. The times are simulated.
512 devices in a mesh: ep: 64 (over x_lo, z, core), blk: 8 (over x_hi, y).
Axes of the slice: x: 4 (x_hi: 2, x_lo: 2; x = x_hi * 2 + x_lo), y: 4, z: 16, core: 2. Of those that a mesh axis runs over, the one named last changes fastest.
Arguments:
- tokens: bfloat16 [4096, 2048], P(('ep', 'blk')), may hold values from -6 to 6
- routes: int32 [4096, 8], P('ep'), may hold values from 0 to 63, all different within a row; in each aligned block of 64 rows (0 to 63, 64 to 127, ...) at most 16 rows name the same one
- gate_scale: bfloat16 [4096, 8], P('ep'), may hold values from 0.099609375 to 1
- placement: int32 [64], replicated, may hold values from 0 to 63, each once
- w_gate: bfloat16 [64, 2048, 1024], P('ep', None, 'blk'), may hold values from -0.125 to 0.125
- w_up: bfloat16 [64, 2048, 1024], P('ep', None, 'blk'), may hold values from -0.125 to 0.125
- w_down: bfloat16 [64, 1024, 2048], P('ep', 'blk'), may hold values from -0.1875 to 0.1875
Outputs:
- mixed: bfloat16 [4096, 2048], P(('ep', 'blk'))
Inputs may be any that keep to these rules, and one draw needn't show every extreme that they name: `routes`: in each aligned block of 64 rows (the tokens of one index of ep) no expert is named by more than 16 rows, a bound that some block reaches; a row names 8 different experts. `placement`: each ep index holds exactly one expert.
All inputs are finite; a program needn't handle non-finite values.
Results may differ from a plain program's by a relative error of at most 0.019.
Values may be sent and summed in bfloat16 or wider, within the bound.
A program may use at most 64 MiB of HBM per device.

v0:
```python
import jax
import jax.numpy as jnp
from jax import lax
from jax.sharding import PartitionSpec as P

TOP = 8


def expert_rows(arrived, w_gate, w_up, w_down):
    row_shape = arrived.shape
    flat_rows = arrived.reshape(-1, row_shape[-1])
    gate_proj = jnp.dot(flat_rows, w_gate[0], preferred_element_type=jnp.float32)
    up_proj = jnp.dot(flat_rows, w_up[0], preferred_element_type=jnp.float32)
    hidden = (jax.nn.silu(gate_proj) * up_proj).astype(jnp.bfloat16)
    output = jnp.dot(hidden, w_down[0], preferred_element_type=jnp.float32).astype(jnp.bfloat16)
    return output.reshape(row_shape)


def local(tokens, routes, gate_scale, placement, w_gate, w_up, w_down):
    ep_count = lax.axis_size("ep")
    blk_count = lax.axis_size("blk")
    own_count = tokens.shape[0]
    width = tokens.shape[1]
    block_size = own_count * blk_count
    capacity = blk_count * max(1, 2 * TOP * own_count // ep_count)
    slots_total = ep_count * capacity
    gathered = lax.all_gather(tokens, "blk", axis=0, tiled=True)
    ep_ids = lax.iota(jnp.int32, ep_count)
    holder = jnp.sum(
        jnp.where(routes[:, :, None] == ep_ids[None, None, :], placement[None, None, :], 0), axis=-1
    )
    flat_holder = holder.reshape(-1)
    onehot = (flat_holder[:, None] == ep_ids[None, :]).astype(jnp.int32)
    before = jnp.cumsum(onehot, axis=0) - onehot
    slot_index = jnp.sum(before * onehot, axis=1)
    position = flat_holder * capacity + slot_index
    matches = (position[None, :] == lax.iota(jnp.int32, slots_total)[:, None]).reshape(
        slots_total, block_size, TOP
    )
    picked = jnp.any(matches, axis=2).astype(jnp.bfloat16)
    buffer = jnp.dot(picked, gathered, preferred_element_type=jnp.float32).astype(jnp.bfloat16)
    buffer = buffer.reshape(ep_count, capacity, width)
    combine_weights = jnp.sum(
        jnp.where(matches, gate_scale[None, :, :], jnp.zeros((), jnp.bfloat16)), axis=2
    )
    finished = None
    arrived = lax.all_to_all(buffer, "ep", split_axis=0, concat_axis=0, tiled=True)
    returned = lax.all_to_all(
        expert_rows(arrived, w_gate, w_up, w_down), "ep", split_axis=0, concat_axis=0, tiled=True
    )
    returned_flat = returned.reshape(slots_total, width)
    combined = lax.dot_general(
        combine_weights, returned_flat, (((0,), (0,)), ((), ())), preferred_element_type=jnp.float32
    )
    summed = lax.psum_scatter(combined.astype(jnp.bfloat16), "blk", scatter_dimension=0, tiled=True)
    finished = summed
    return finished


def solution(mesh):
    in_specs = (
        P(("ep", "blk"), None),
        P("ep", None),
        P("ep", None),
        P(),
        P("ep", None, "blk"),
        P("ep", None, "blk"),
        P("ep", "blk", None),
    )
    out_specs = P(("ep", "blk"), None)
    return jax.shard_map(local, mesh=mesh, in_specs=in_specs, out_specs=out_specs, check_vma=False)
```

profile of v0, /device:TPU:6, one launch (start us, length us, event | category | flops | bytes accessed | tf_op | source)
XLA Modules:
  0.0 550.2 jit_solution(13190970564214001270)
XLA Ops:
  6.5 0.0 copy-start
  6.5 0.8 copy.13
  7.4 1.9 select_reduce_fusion
  9.3 0.1 eq.59
  9.4 0.1 eq.55
  9.5 1.2 reduce-window.6
  10.7 0.2 slice_reduce_fusion
  10.9 0.1 fusion.17
  11.1 0.1 reduce_sum.34
  11.2 0.7 fusion
  11.9 34.7 %all_gather.3 = bf16[64,2048]{1,0:T(8,128)(2,1)S(1)} all-gather(bf16[8,2048]{1,0:T(8,128)(2,1)} %param.7), channel_id=1, replica_groups=mesh['ep'=64,'blk'=8] {'blk'}, dimensions={0}, use_global_device_ids=true | all-gather | bytes 294912 | tf_op jit(solution)/shard_map/all_gather | solution.py:27
  46.6 1.3 convolution_convert_fusion.1
  47.9 0.0 copy-start.2
  48.0 203.5 %all_to_all.10 = bf16[64,16,2048]{2,1,0:T(8,128)(2,1)S(1)} all-to-all(bf16[64,16,2048]{2,1,0:T(8,128)(2,1)S(1)} %bitcast.42), channel_id=1, replica_groups=mesh['ep'=64,'blk'=8] {'ep'}, dimensions={0} | all-to-all | bytes 8388608 | tf_op jit(solution)/shard_map/all_to_all | solution.py:47
  251.5 0.0 copy-start.1
  251.5 0.0 copy-start.3
  251.5 1.9 copy-done.1
  253.4 0.0 copy-done.2
  253.4 1.2 fusion.7
  254.7 0.0 copy-done
  254.7 0.0 copy-done.3
  254.7 8.5 %convolution_convert_fusion = bf16[1024,2048]{1,0:T(8,128)(2,1)} fusion(bf16[1024,2048]{1,0:T(8,128)(2,1)} %bitcast.40, bf16[1,128,2048]{2,1,0:T(8,128)(2,1)S(1)} %copy-done, bf16[1,2048,128]{2,1,0:T(8,128)(2,1)S(1)} %copy-done.3, f32[1024,128]{1,0:T(8,128)S(1)} %fusion.7), kind=kOutput, calls=%fused_computation | convolution fusion | flops 1076625408 | bytes 9961472 | tf_op jit(solution)/shard_map/dot_general | solution.py:15
  263.2 0.0 copy-start.4
  263.2 8.7 %all-to-all-start.1 = ((bf16[64,16,2048]{2,1,0:T(8,128)(2,1)}), bf16[64,16,2048]{2,1,0:T(8,128)(2,1)}, u32[]{:S(2)}, u32[]{:S(2)}) async-start(bf16[64,16,2048]{2,1,0:T(8,128)(2,1)} %bitcast.41), calls=%async_computation.1 | async-start | bytes 8388608 | tf_op jit(solution)/shard_map/all_to_all | solution.py:48
  271.9 0.0 reduce-scatter.2.cloned.1.call-start
  272.0 0.0 copy-done.4
  272.0 0.1 copy.15
  272.1 0.7 fusion.3
  272.8 187.6 %all-to-all-done.1 = bf16[64,16,2048]{2,1,0:T(8,128)(2,1)} async-done(((bf16[64,16,2048]{2,1,0:T(8,128)(2,1)}), bf16[64,16,2048]{2,1,0:T(8,128)(2,1)}, u32[]{:S(2)}, u32[]{:S(2)}) %all-to-all-start.1) | async-done | bytes 4194336 | tf_op jit(solution)/shard_map/all_to_all | solution.py:48
  460.4 3.7 convolution_convert_fusion.2
  464.1 0.0 reduce-scatter.2.cloned.1.call-update
  464.2 79.2 %reduce-scatter.2.cloned.1.call-done = bf16[8,2048]{1,0:T(8,128)(2,1)} async-done(((bf16[64,2048]{1,0:T(8,128)(2,1)}), bf16[8,2048]{1,0:T(8,128)(2,1)}) %reduce-scatter.2.cloned.1.call-update) | async-done | bytes 32784 | tf_op jit(solution)/shard_map/reduce_scatter | solution.py:55
  (4 shorter events, 0.1 us)
Async XLA Ops:
  6.5 248.1 %copy-start = (bf16[1,128,2048]{2,1,0:T(8,128)(2,1)S(1)}, bf16[1,128,2048]{2,1,0:T(8,128)(2,1)}, u32[]{:S(2)}) copy-start(bf16[1,128,2048]{2,1,0:T(8,128)(2,1)} %param.13) | copy-start | bytes 1572868
  47.9 205.5 %copy-start.2 = (bf16[1,2048,128]{2,1,0:T(8,128)(2,1)S(1)}, bf16[1,2048,128]{2,1,0:T(8,128)(2,1)}, u32[]{:S(2)}) copy-start(bf16[1,2048,128]{2,1,0:T(8,128)(2,1)} %param.11) | copy-start | bytes 1572868
  251.5 1.9 copy-start.1
  251.5 3.2 copy-start.3
  263.2 8.8 %copy-start.4 = (bf16[64,8]{0,1:T(8,128)(2,1)S(1)}, bf16[64,8]{0,1:T(8,128)(2,1)}, u32[]{:S(2)}) copy-start(bf16[64,8]{0,1:T(8,128)(2,1)} %param.9) | copy-start | bytes 3076
  263.2 197.2 %all-to-all-start.1 = ((bf16[64,16,2048]{2,1,0:T(8,128)(2,1)}), bf16[64,16,2048]{2,1,0:T(8,128)(2,1)}, u32[]{:S(2)}, u32[]{:S(2)}) async-start(bf16[64,16,2048]{2,1,0:T(8,128)(2,1)} %bitcast.41), calls=%async_computation.1 | async-start | bytes 8388608 | tf_op jit(solution)/shard_map/all_to_all | solution.py:48
  271.9 271.4 %reduce-scatter.2.cloned.1.call-start = ((), (), s32[]{:S(2)}) async-start(), calls=%async_computation.3 | async-start | bytes 294912 | tf_op jit(solution)/shard_map/reduce_scatter | solution.py:55
Sparse Core Ops, SparseCore 0:
  464.3 79.0 reduce-scatter.1
where the time goes:
time: 551 us; the launch traced here: 550 us
  waiting for transfers between devices  267 us (48%)
  blocking collectives  238 us (43%)
  matrix products  14.8 us (3%)
  between operations  13.5 us (2%)
  starting transfers between devices  8.76 us (2%)
    all_to_all x1, blocking collectives, local(): lax.all_to_all(buffer, 'ep', split_axis=0, concat_axis=0, tiled=True)  204 us
    all_to_all x1, waiting for transfers between devices, local(): lax.all_to_all(expert_rows(arrived, w_gate, w_up, w_down), 'ep', split_ax...  188 us
    reduce_scatter x1, waiting for transfers between devices, local(): lax.psum_scatter(combined.astype(jnp.bfloat16), 'blk', scatter_dimension=...  79.2 us
    all_gather x1, blocking collectives, local(): gathered = lax.all_gather(tokens, 'blk', axis=0, tiled=True)  34.7 us
  transfers between devices with their start and end apart: 2, of which 2 were waited for; matrix products, arithmetic and copies ran while one was open for 0% of the time, Pallas kernels for 0%

commit v1 on v0

v1 whole, which is shorter than its diff:
```python
import jax
import jax.numpy as jnp
from jax import lax
from jax.sharding import Mesh, PartitionSpec as P

AXES = ("xl", "z", "core", "xh", "y")
EP = ("xl", "z", "core")
BLK = ("xh", "y")
PLANE = ("y", "xh", "xl", "z")


def local(tokens, routes, gate_scale, placement, w_gate, w_up, w_down):
    own = tokens.shape[0]
    experts = placement.shape[0]
    blk_index = lax.axis_index("xh") * lax.axis_size("y") + lax.axis_index("y")
    my_routes = lax.dynamic_slice_in_dim(routes, blk_index * own, own, 0)
    my_scale = lax.dynamic_slice_in_dim(gate_scale, blk_index * own, own, 0)
    ids = lax.iota(jnp.int32, experts)
    chosen = my_routes[:, :, None] == ids[None, None, :]
    holder = jnp.sum(jnp.where(chosen, placement[None, None, :], 0), axis=-1)
    dense = jnp.sum(
        jnp.where(holder[:, :, None] == ids[None, None, :], my_scale[:, :, None].astype(jnp.float32), 0.0), axis=1
    ).astype(jnp.bfloat16)
    packed = jnp.concatenate([tokens, dense, jnp.zeros_like(dense)], axis=1)
    everyone = lax.all_gather(packed, "z", axis=0, tiled=True)
    everyone = lax.all_gather(everyone, ("xh", "xl"), axis=0, tiled=True)
    everyone = lax.all_gather(everyone, "y", axis=0, tiled=True)
    width = tokens.shape[1]
    x = everyone[:, :width]
    weights = everyone[:, width : width + experts]
    swap = [(0, 1), (1, 0)]
    wg = jnp.concatenate([w_gate[0], lax.ppermute(w_gate[0], "core", swap)], axis=1)
    wu = jnp.concatenate([w_up[0], lax.ppermute(w_up[0], "core", swap)], axis=1)
    wd = jnp.concatenate([w_down[0], lax.ppermute(w_down[0], "core", swap)], axis=0)
    core = lax.axis_index("core")
    pair = (lax.axis_index("xl") * lax.axis_size("z") + lax.axis_index("z")) * 2
    mine = lax.dynamic_slice_in_dim(weights, pair + core, 1, 1).astype(jnp.float32)
    other = lax.dynamic_slice_in_dim(weights, pair + 1 - core, 1, 1).astype(jnp.float32)
    half = w_down.shape[1]
    first = lax.broadcasted_iota(jnp.int32, (1, 2 * half), 1) < half
    scale = jnp.where(first, mine, other)
    gate = jnp.dot(x, wg, preferred_element_type=jnp.float32)
    up = jnp.dot(x, wu, preferred_element_type=jnp.float32)
    hidden = (jax.nn.silu(gate) * up * scale).astype(jnp.bfloat16)
    out = jnp.dot(hidden, wd, preferred_element_type=jnp.float32).astype(jnp.bfloat16)
    part = lax.psum_scatter(out, "y", scatter_dimension=0, tiled=True)
    part = lax.optimization_barrier(lax.psum_scatter(part, ("xh", "xl"), scatter_dimension=0, tiled=True).astype(jnp.float32))
    total = lax.psum_scatter(part, "z", scatter_dimension=0, tiled=True)
    return lax.optimization_barrier(total).astype(jnp.bfloat16)


def solution(mesh):
    fine = Mesh(mesh.devices.reshape(2, 16, 2, 2, 4), AXES)
    in_specs = (
        P(AXES, None),
        P(EP, None),
        P(EP, None),
        P(),
        P(EP, None, BLK),
        P(EP, None, BLK),
        P(EP, BLK, None),
    )
    return jax.shard_map(local, mesh=fine, in_specs=in_specs, out_specs=P(AXES, None), check_vma=False)
```

time: 551 us -> 418 us (0.76)
  blocking collectives: 238 us -> 40.7 us
  waiting for transfers between devices: 267 us -> 328 us
  matrix products: 14.8 us -> 20.4 us
    all_to_all x1 -> x0, blocking collectives: 204 us -> none  [local(): lax.all_to_all(buffer, 'ep', split_axis=0, concat_axis=0, tiled=True)]
    all_to_all x1 -> x0, waiting for transfers between devices: 188 us -> none  [local(): lax.all_to_all(expert_rows(arrived, w_gate, w_up, w_down), 'ep', split_ax...]
    all_gather x0 -> x2, waiting for transfers between devices: none -> 127 us  [the longest x1 92.9 us: local(): everyone = lax.all_gather(everyone, 'y', axis=0, tiled=True)]
    reduce_scatter x1 -> x3, waiting for transfers between devices: 79.2 us -> 201 us  [the longest x1 89.4 us: local(): part = lax.psum_scatter(out, 'y', scatter_dimension=0, tiled=True)]
    all_to_all x1 -> x0, starting transfers between devices: 8.72 us -> none  [local(): lax.all_to_all(expert_rows(arrived, w_gate, w_up, w_down), 'ep', split_ax...]
    ppermute x0 -> x3, starting transfers between devices: none -> 6.25 us  [the longest x1 2.41 us: local(): lax.ppermute(w_gate[0], 'core', swap)]
    all_gather x1, blocking collectives: 34.7 us -> 40.7 us  [local(): everyone = lax.all_gather(packed, 'z', axis=0, tiled=True)]
    dot_general x4 -> x2, matrix products: 14.8 us -> 20.4 us  [the longest x1 13.3 us: local(): jnp.dot(hidden, wd, preferred_element_type=jnp.float32).astype(jnp.bfloat16)]
  transfers between devices with their start and end apart: 2 -> 8, of which waited for: 2 -> 5; matrix products, arithmetic and copies ran while one was open for 0% -> 2% of each run, Pallas kernels for 0% -> 0%
where the time goes in v1:
time: 418 us
  waiting for transfers between devices  328 us (78%)
  blocking collectives  40.7 us (10%)
  matrix products  20.4 us (5%)
  between operations  13.3 us (3%)
  starting transfers between devices  6.44 us (2%)
  other arithmetic  6.1 us (1%)
    all_gather x1, waiting for transfers between devices, local(): everyone = lax.all_gather(everyone, 'y', axis=0, tiled=True)  92.9 us
    reduce_scatter x1, waiting for transfers between devices, local(): part = lax.psum_scatter(out, 'y', scatter_dimension=0, tiled=True)  89.4 us
    reduce_scatter x1, waiting for transfers between devices, local(): total = lax.psum_scatter(part, 'z', scatter_dimension=0, tiled=True)  73.6 us
    all_gather x1, blocking collectives, local(): everyone = lax.all_gather(packed, 'z', axis=0, tiled=True)  40.7 us
    reduce_scatter x1, waiting for transfers between devices, local(): lax.psum_scatter(part, ('xh', 'xl'), scatter_dimension=0, tiled=True)  37.9 us
    all_gather x1, waiting for transfers between devices, local(): everyone = lax.all_gather(everyone, ('xh', 'xl'), axis=0, tiled=True)  34 us
    dot_general x1, matrix products, local(): jnp.dot(hidden, wd, preferred_element_type=jnp.float32).astype(jnp.bfloat16)  13.3 us
  transfers between devices with their start and end apart: 8, of which 5 were waited for; matrix products, arithmetic and copies ran while one was open for 2% of the time, Pallas kernels for 0%

profile of v1, /device:TPU:6, one launch (start us, length us, event | category | flops | bytes accessed | tf_op | source)
XLA Modules:
  0.0 417.5 jit_solution(12385986493303225261)
XLA Ops:
  6.5 0.0 all-gather.3.cloned.1.call-start
  6.6 0.6 copy-done
  7.2 0.1 constant_dynamic-slice_fusion
  7.3 0.1 copy.12
  7.4 0.8 dynamic-slice_convert_fusion
  8.1 0.1 copy.13
  8.2 0.9 select_reduce_fusion.1
  9.1 0.1 select_reduce_fusion
  9.2 0.8 concatenate.12
  10.1 40.7 %all_gather.9 = bf16[128,2176]{1,0:T(8,128)(2,1)} all-gather(bf16[8,2176]{1,0:T(8,128)(2,1)S(1)} %concatenate.12), channel_id=1, replica_groups=mesh['xl'=2,'z'=16,'core'=2,'xh'=2,'y'=4] {'z'}, dimensions={0}, use_global_device_ids=true | all-gather | bytes 591872 | tf_op jit(solution)/shard_map/all_gather | solution.py:25
  50.8 0.0 all-gather.3.cloned.1.call-update
  50.8 0.0 all-gather.5.cloned.1.call-start
  50.8 34.0 %all-gather.3.cloned.1.call-done = bf16[512,2176]{1,0:T(8,128)(2,1)} async-done(((bf16[128,2176]{1,0:T(8,128)(2,1)}), bf16[512,2176]{1,0:T(8,128)(2,1)}) %all-gather.3.cloned.1.call-update) | async-done | bytes 2228240 | tf_op jit(solution)/shard_map/all_gather | solution.py:26
  84.9 0.0 all-gather.5.cloned.1.call-update
  84.9 0.0 reduce-scatter.4.cloned.1.call-start
  84.9 1.9 collective-permute-start.1
  86.9 2.4 collective-permute-start
  89.3 1.9 collective-permute-start.2
  91.3 92.9 %all-gather.5.cloned.1.call-done = bf16[2048,2176]{1,0:T(8,128)(2,1)} async-done(((bf16[512,2176]{1,0:T(8,128)(2,1)}), bf16[2048,2176]{1,0:T(8,128)(2,1)}) %all-gather.5.cloned.1.call-update) | async-done | bytes 8912912 | tf_op jit(solution)/shard_map/all_gather | solution.py:27
  184.1 1.1 slice.9
  185.2 0.7 convert_reduce_fusion.1
  186.0 7.1 %fusion = f32[2048,256]{1,0:T(8,128)} fusion(bf16[2048,2176]{1,0:T(8,128)(2,1)} %all-gather.5.cloned.1.call-done, bf16[2048,128]{1,0:T(8,128)(2,1)S(1)} %collective-permute-done.1, bf16[2048,128]{1,0:T(8,128)(2,1)S(1)} %bitcast.4), kind=kOutput, calls=%fused_computation.1 | convolution fusion | flops 2149580800 | bytes 11534336 | tf_op jit(solution)/shard_map/dot_general | solution.py:43
  193.1 13.3 %convolution_convert_fusion = bf16[2048,2048]{1,0:T(8,128)(2,1)} fusion(f32[2048,256]{1,0:T(8,128)} %fusion, bf16[128,2048]{1,0:T(8,128)(2,1)S(1)} %collective-permute-done.2, bf16[128,2048]{1,0:T(8,128)(2,1)S(1)} %bitcast.6, f32[2048]{0:T(1024)S(1)} %get-tuple-element.6, f32[2048]{0:T(1024)S(1)} %get-tuple-element.5, ...), kind=kOutput, calls=%fused_computation | convolution fusion | flops 4307550208 | bytes 20988160 | tf_op jit(solution)/shard_map/dot_general | solution.py:45
  206.3 0.0 reduce-scatter.4.cloned.1.call-update
  206.3 0.0 reduce-scatter.6.cloned.1.call-start
  206.4 89.4 %reduce-scatter.4.cloned.1.call-done = bf16[512,2048]{1,0:T(8,128)(2,1)} async-done(((bf16[2048,2048]{1,0:T(8,128)(2,1)}), bf16[512,2048]{1,0:T(8,128)(2,1)}) %reduce-scatter.4.cloned.1.call-update) | async-done | bytes 2097168 | tf_op jit(solution)/shard_map/reduce_scatter | solution.py:46
  295.8 0.0 reduce-scatter.8.cloned.1.call-start
  295.9 37.9 %reduce-scatter.6.cloned.1.call-done = bf16[128,2048]{1,0:T(8,128)(2,1)} async-done(((bf16[512,2048]{1,0:T(8,128)(2,1)}), bf16[128,2048]{1,0:T(8,128)(2,1)}) %reduce-scatter.6.cloned.1.call-update) | async-done | bytes 524304 | tf_op jit(solution)/shard_map/reduce_scatter | solution.py:47
  333.8 2.1 convert_element_type.25
  335.9 0.0 reduce-scatter.8.cloned.1.call-update
  335.9 73.6 %reduce-scatter.8.cloned.1.call-done = f32[8,2048]{1,0:T(8,128)} async-done(((f32[128,2048]{1,0:T(8,128)}), f32[8,2048]{1,0:T(8,128)}) %reduce-scatter.8.cloned.1.call-update) | async-done | bytes 65552 | tf_op jit(solution)/shard_map/reduce_scatter | solution.py:48
  409.5 1.5 convert_element_type.26
  (13 shorter events, 0.0 us)
Async XLA Ops:
  6.5 0.7 copy-start
  6.5 78.4 %copy-start.1 = (bf16[1,2048,128]{2,1,0:T(8,128)(2,1)S(1)}, bf16[1,2048,128]{2,1,0:T(8,128)(2,1)}, u32[]{:S(2)}) copy-start(bf16[1,2048,128]{2,1,0:T(8,128)(2,1)} %param.12) | copy-start | bytes 1572868
  6.5 80.3 %copy-start.3 = (bf16[1,2048,128]{2,1,0:T(8,128)(2,1)S(1)}, bf16[1,2048,128]{2,1,0:T(8,128)(2,1)}, u32[]{:S(2)}) copy-start(bf16[1,2048,128]{2,1,0:T(8,128)(2,1)} %param.11) | copy-start | bytes 1572868
  6.5 82.7 %copy-start.2 = (bf16[1,128,2048]{2,1,0:T(8,128)(2,1)S(1)}, bf16[1,128,2048]{2,1,0:T(8,128)(2,1)}, u32[]{:S(2)}) copy-start(bf16[1,128,2048]{2,1,0:T(8,128)(2,1)} %param.13) | copy-start | bytes 1572868
  6.5 78.3 %all-gather.3.cloned.1.call-start = ((), (), s32[]{:S(2)}) async-start(), calls=%async_computation.3 | async-start | bytes 2785280 | tf_op jit(solution)/shard_map/all_gather | solution.py:26
  50.8 133.3 %all-gather.5.cloned.1.call-start = ((), (), s32[]{:S(2)}) async-start(), calls=%async_computation.4 | async-start | bytes 11141120 | tf_op jit(solution)/shard_map/all_gather | solution.py:27
  84.9 210.9 %reduce-scatter.4.cloned.1.call-start = ((), (), s32[]{:S(2)}) async-start(), calls=%async_computation.5 | async-start | bytes 10485760 | tf_op jit(solution)/shard_map/reduce_scatter | solution.py:46
  84.9 101.0 %collective-permute-start.1 = (bf16[2048,128]{1,0:T(8,128)(2,1)S(1)}, bf16[2048,128]{1,0:T(8,128)(2,1)S(1)}, u32[]{:S(2)}, u32[]{:S(2)}) collective-permute-start(bf16[2048,128]{1,0:T(8,128)(2,1)S(1)} %bitcast.3), channel_id=1, source_target_pairs={{0,8},{8,0},{1,9},{9,1},{2,10},{10,2},{3,11},{11,3},{4,12},{12,4},... | collective-permute-start | bytes 1572872 | tf_op jit(solution)/shard_map/ppermute | solution.py:33
  86.9 106.2 %collective-permute-start = (bf16[2048,128]{1,0:T(8,128)(2,1)S(1)}, bf16[2048,128]{1,0:T(8,128)(2,1)S(1)}, u32[]{:S(2)}, u32[]{:S(2)}) collective-permute-start(bf16[2048,128]{1,0:T(8,128)(2,1)S(1)} %bitcast.7), channel_id=1, source_target_pairs={{0,8},{8,0},{1,9},{9,1},{2,10},{10,2},{3,11},{11,3},{4,12},{12,4},... | collective-permute-start | bytes 1572872 | tf_op jit(solution)/shard_map/ppermute | solution.py:32
  89.3 103.8 %collective-permute-start.2 = (bf16[128,2048]{1,0:T(8,128)(2,1)S(1)}, bf16[128,2048]{1,0:T(8,128)(2,1)S(1)}, u32[]{:S(2)}, u32[]{:S(2)}) collective-permute-start(bf16[128,2048]{1,0:T(8,128)(2,1)S(1)} %bitcast.5), channel_id=1, source_target_pairs={{0,8},{8,0},{1,9},{9,1},{2,10},{10,2},{3,11},{11,3},{4,12},{12,4},... | collective-permute-start | bytes 1572872 | tf_op jit(solution)/shard_map/ppermute | solution.py:34
  206.3 127.5 %reduce-scatter.6.cloned.1.call-start = ((), (), s32[]{:S(2)}) async-start(), calls=%async_computation.6 | async-start | bytes 2621440 | tf_op jit(solution)/shard_map/reduce_scatter | solution.py:47
  295.8 113.7 %reduce-scatter.8.cloned.1.call-start = ((), (), s32[]{:S(2)}) async-start(), calls=%async_computation.7 | async-start | bytes 1114112 | tf_op jit(solution)/shard_map/reduce_scatter | solution.py:48
Sparse Core Ops, SparseCore 0:
  50.9 33.8 all-gather.2
  86.9 97.1 all-gather.4
  206.5 89.2 reduce-scatter.3
  298.5 35.2 reduce-scatter.5
  336.5 73.0 reduce-scatter.7

commit v2 on v1

--- a/solution.py
+++ b/solution.py
@@ -6,7 +6,45 @@
 AXES = ("xl", "z", "core", "xh", "y")
 EP = ("xl", "z", "core")
 BLK = ("xh", "y")
-PLANE = ("y", "xh", "xl", "z")
+
+
+X = ("xl", "xh")
+PLACE = {X: (0, 2, 1, 3), "y": (0, 1, 2, 3)}
+
+
+def step(v, axis, by):
+    place = PLACE[axis]
+    return lax.ppermute(v, axis, [(place[i], place[(i + by) % 4]) for i in range(4)])
+
+
+def ring_gather(v, axis):
+    half = v.shape[0] // 2
+    left = step(v, axis, 1)
+    right = step(v, axis, -1)
+    return jnp.concatenate([v, left, right, step(left[:half], axis, 1), step(right[half:], axis, -1)], axis=0)
+
+
+def add(a, b):
+    return (a.astype(jnp.float32) + b.astype(jnp.float32)).astype(jnp.bfloat16)
+
+
+def ring_scatter(v, axis):
+    rows = v.shape[0] // 4
+    half = rows // 2
+    own, left, right, far = (v[k * rows : (k + 1) * rows] for k in range(4))
+    from_left = step(far[:half], axis, 1)
+    from_right = step(far[half:], axis, -1)
+    below = step(right[half:], axis, 1)
+    above = step(left[:half], axis, -1)
+    first = step(add(right[:half], from_left), axis, 1)
+    second = step(add(left[half:], from_right), axis, -1)
+    one = jnp.concatenate([first, below], axis=0).astype(jnp.float32)
+    two = jnp.concatenate([above, second], axis=0).astype(jnp.float32)
+    return own.astype(jnp.float32) + one + two
+
+
+def swapped(v):
+    return v.reshape(4, 4, v.shape[0] // 16, v.shape[1]).transpose(1, 0, 2, 3).reshape(v.shape)
 
 
 def local(tokens, routes, gate_scale, placement, w_gate, w_up, w_down):
@@ -21,13 +59,15 @@
     dense = jnp.sum(
         jnp.where(holder[:, :, None] == ids[None, None, :], my_scale[:, :, None].astype(jnp.float32), 0.0), axis=1
     ).astype(jnp.bfloat16)
-    packed = jnp.concatenate([tokens, dense, jnp.zeros_like(dense)], axis=1)
+    packed = jnp.concatenate([dense, jnp.zeros_like(dense), tokens], axis=1)
     everyone = lax.all_gather(packed, "z", axis=0, tiled=True)
-    everyone = lax.all_gather(everyone, ("xh", "xl"), axis=0, tiled=True)
-    everyone = lax.all_gather(everyone, "y", axis=0, tiled=True)
     width = tokens.shape[1]
-    x = everyone[:, :width]
-    weights = everyone[:, width : width + experts]
+    pad = 2 * experts
+    cut = pad + width // 2
+    part_a = ring_gather(ring_gather(everyone[:, :cut], X), "y")
+    part_b = swapped(ring_gather(ring_gather(everyone[:, cut:], "y"), X))
+    x = jnp.concatenate([part_a[:, pad:], part_b], axis=1)
+    weights = part_a[:, :experts]
     swap = [(0, 1), (1, 0)]
     wg = jnp.concatenate([w_gate[0], lax.ppermute(w_gate[0], "core", swap)], axis=1)
     wu = jnp.concatenate([w_up[0], lax.ppermute(w_up[0], "core", swap)], axis=1)
@@ -43,8 +83,10 @@
     up = jnp.dot(x, wu, preferred_element_type=jnp.float32)
     hidden = (jax.nn.silu(gate) * up * scale).astype(jnp.bfloat16)
     out = jnp.dot(hidden, wd, preferred_element_type=jnp.float32).astype(jnp.bfloat16)
-    part = lax.psum_scatter(out, "y", scatter_dimension=0, tiled=True)
-    part = lax.optimization_barrier(lax.psum_scatter(part, ("xh", "xl"), scatter_dimension=0, tiled=True).astype(jnp.float32))
+    out_a, out_b = out[:, : width // 2], swapped(out[:, width // 2 :])
+    sum_a = ring_scatter(ring_scatter(out_a, "y").astype(jnp.bfloat16), X)
+    sum_b = ring_scatter(ring_scatter(out_b, X).astype(jnp.bfloat16), "y")
+    part = lax.optimization_barrier(jnp.concatenate([sum_a, sum_b], axis=1))
     total = lax.psum_scatter(part, "z", scatter_dimension=0, tiled=True)
     return lax.optimization_barrier(total).astype(jnp.bfloat16)
 

time: 418 us -> 324 us (0.78)
  waiting for transfers between devices: 328 us -> 88.6 us
  starting transfers between devices: 6.44 us -> 137 us
  local copies, waits for them, and re-layouts: 2.78 us -> 27.4 us
  matrix products: 20.4 us -> 8.94 us
    ppermute x0 -> x40, starting transfers between devices: none -> 130 us  [step(): lax.ppermute(v, axis, [(place[i], place[(i + by) % 4]) for i in range(4)])]
    reduce_scatter x2 -> x0, waiting for transfers between devices: 127 us -> none  [the longest x1 89.4 us: local(): part = lax.psum_scatter(out, 'y', scatter_dimension=0, tiled=True)]
    all_gather x2 -> x0, waiting for transfers between devices: 127 us -> none  [the longest x1 92.9 us: local(): everyone = lax.all_gather(everyone, 'y', axis=0, tiled=True)]
    ppermute x0 -> x40, waiting for transfers between devices: none -> 22.3 us  [step(): lax.ppermute(v, axis, [(place[i], place[(i + by) % 4]) for i in range(4)])]
    unnamed x8 -> x22, local copies, waits for them, and re-layouts: 0.64 us -> 14.2 us
    dot_general x1, matrix products: 13.3 us -> 2.84 us  [local(): jnp.dot(hidden, wd, preferred_element_type=jnp.float32).astype(jnp.bfloat16)]
    reduce_scatter x1, waiting for transfers between devices: 73.6 us -> 66.2 us  [local(): total = lax.psum_scatter(part, 'z', scatter_dimension=0, tiled=True)]
    slice x1 -> x16, local copies, waits for them, and re-layouts: 1.08 us -> 6.28 us  [the longest x1 2.63 us: local(): x = jnp.concatenate([part_a[:, pad:], part_b], axis=1)]
  transfers between devices with their start and end apart: 8 -> 44, of which waited for: 5 -> 11; matrix products, arithmetic and copies ran while one was open for 2% -> 10% of each run, Pallas kernels for 0% -> 0%
where the time goes in v2:
time: 324 us; the launch traced here: 322 us
  starting transfers between devices  137 us (42%)
  waiting for transfers between devices  88.6 us (27%)
  blocking collectives  38.7 us (12%)
  local copies, waits for them, and re-layouts  27.4 us (8%)
  between operations  14.2 us (4%)
  matrix products  8.94 us (3%)
  other arithmetic  7.52 us (2%)
    ppermute x40, starting transfers between devices, step(): lax.ppermute(v, axis, [(place[i], place[(i + by) % 4]) for i in range(4)])  130 us
    reduce_scatter x1, waiting for transfers between devices, local(): total = lax.psum_scatter(part, 'z', scatter_dimension=0, tiled=True)  66.2 us
    all_gather x1, blocking collectives, local(): everyone = lax.all_gather(packed, 'z', axis=0, tiled=True)  38.7 us
    ppermute x40, waiting for transfers between devices, step(): lax.ppermute(v, axis, [(place[i], place[(i + by) % 4]) for i in range(4)])  22.3 us
    unnamed x22, local copies, waits for them, and re-layouts  14.2 us
  transfers between devices with their start and end apart: 44, of which 11 were waited for; matrix products, arithmetic and copies ran while one was open for 10% of the time, Pallas kernels for 0%

profile of v2, /device:TPU:6, one launch (start us, length us, event | category | flops | bytes accessed | tf_op | source)
XLA Modules:
  0.0 322.2 jit_solution(18180294865599088376)
XLA Ops:
  9.4 38.7 %all_gather.3 = bf16[128,2176]{1,0:T(8,128)(2,1)S(1)} all-gather(bf16[8,2176]{1,0:T(8,128)(2,1)S(1)} %concatenate.56), channel_id=1, replica_groups=mesh['xl'=2,'z'=16,'core'=2,'xh'=2,'y'=4] {'z'}, dimensions={0}, use_global_device_ids=true | all-gather | bytes 591872 | tf_op jit(solution)/shard_map/all_gather | solution.py:63
  49.0 3.5 %collective-permute-start.8 = (bf16[128,1024]{1,0:T(8,128)(2,1)S(1)}, bf16[128,1024]{1,0:T(8,128)(2,1)S(1)}, u32[]{:S(2)}, u32[]{:S(2)}) collective-permute-start(bf16[128,1024]{1,0:T(8,128)(2,1)S(1)} %get-tuple-element.36), channel_id=1, source_target_pairs={{0,1},{1,2},{2,3},{3,0},{4,5},{5,6},{6,7},{7,4},{8,9},{9,10},{10,1... | collective-permute-start | bytes 786440 | tf_op jit(solution)/shard_map/ppermute | solution.py:17
  52.5 3.6 %collective-permute-start.9 = (bf16[128,1024]{1,0:T(8,128)(2,1)S(1)}, bf16[128,1024]{1,0:T(8,128)(2,1)S(1)}, u32[]{:S(2)}, u32[]{:S(2)}) collective-permute-start(bf16[128,1024]{1,0:T(8,128)(2,1)S(1)} %get-tuple-element.36), channel_id=1, source_target_pairs={{0,3},{1,0},{2,1},{3,2},{4,7},{5,4},{6,5},{7,6},{8,11},{9,8},{10,9... | collective-permute-start | bytes 786440 | tf_op jit(solution)/shard_map/ppermute | solution.py:17
  59.3 3.5 %collective-permute-start.1 = (bf16[128,1152]{1,0:T(8,128)(2,1)S(1)}, bf16[128,1152]{1,0:T(8,128)(2,1)S(1)}, u32[]{:S(2)}, u32[]{:S(2)}) collective-permute-start(bf16[128,1152]{1,0:T(8,128)(2,1)S(1)} %get-tuple-element.33), channel_id=1, source_target_pairs={{0,260},{256,0},{4,256},{260,4},{1,261},{257,1},{5,257},{261,5},{2... | collective-permute-start | bytes 884744 | tf_op jit(solution)/shard_map/ppermute | solution.py:17
  65.1 4.8 %collective-permute-start.11 = (bf16[64,1024]{1,0:T(8,128)(2,1)S(1)}, bf16[64,1024]{1,0:T(8,128)(2,1)S(1)}, u32[]{:S(2)}, u32[]{:S(2)}) collective-permute-start(bf16[64,1024]{1,0:T(8,128)(2,1)S(1)} %slice.235), channel_id=1, source_target_pairs={{0,3},{1,0},{2,1},{3,2},{4,7},{5,4},{6,5},{7,6},{8,11},{9,8},{10,9... | collective-permute-start | bytes 393224 | tf_op jit(solution)/shard_map/ppermute | solution.py:17
  71.7 3.6 %collective-permute-start.2 = (bf16[64,1152]{1,0:T(8,128)(2,1)S(1)}, bf16[64,1152]{1,0:T(8,128)(2,1)S(1)}, u32[]{:S(2)}, u32[]{:S(2)}) collective-permute-start(bf16[64,1152]{1,0:T(8,128)(2,1)S(1)} %slice.228), channel_id=1, source_target_pairs={{0,256},{256,4},{4,260},{260,0},{1,257},{257,5},{5,261},{261,1},{2... | collective-permute-start | bytes 442376 | tf_op jit(solution)/shard_map/ppermute | solution.py:17
  80.8 4.8 %collective-permute-start.12 = (bf16[512,1024]{1,0:T(8,128)(2,1)}, bf16[512,1024]{1,0:T(8,128)(2,1)S(1)}, u32[]{:S(2)}, u32[]{:S(2)}) collective-permute-start(bf16[512,1024]{1,0:T(8,128)(2,1)} %get-tuple-element.49), channel_id=1, source_target_pairs={{0,256},{256,4},{4,260},{260,0},{1,257},{257,5},{5,261},{261,1},{2... | collective-permute-start | bytes 3145736 | tf_op jit(solution)/shard_map/ppermute | solution.py:17
  90.9 5.1 %collective-permute-start.5 = (bf16[512,1152]{1,0:T(8,128)(2,1)}, bf16[512,1152]{1,0:T(8,128)(2,1)S(1)}, u32[]{:S(2)}, u32[]{:S(2)}) collective-permute-start(bf16[512,1152]{1,0:T(8,128)(2,1)} %get-tuple-element.45), channel_id=1, source_target_pairs={{0,3},{1,0},{2,1},{3,2},{4,7},{5,4},{6,5},{7,6},{8,11},{9,8},{10,9... | collective-permute-start | bytes 3538952 | tf_op jit(solution)/shard_map/ppermute | solution.py:17
  100.2 5.5 %collective-permute-start.14 = (bf16[256,1024]{1,0:T(8,128)(2,1)S(1)}, bf16[256,1024]{1,0:T(8,128)(2,1)S(1)}, u32[]{:S(2)}, u32[]{:S(2)}) collective-permute-start(bf16[256,1024]{1,0:T(8,128)(2,1)S(1)} %slice.236), channel_id=1, source_target_pairs={{0,256},{256,4},{4,260},{260,0},{1,257},{257,5},{5,261},{261,1},{2... | collective-permute-start | bytes 1572872 | tf_op jit(solution)/shard_map/ppermute | solution.py:17
  114.3 5.1 %collective-permute-start.7 = (bf16[256,1152]{1,0:T(8,128)(2,1)S(1)}, bf16[256,1152]{1,0:T(8,128)(2,1)S(1)}, u32[]{:S(2)}, u32[]{:S(2)}) collective-permute-start(bf16[256,1152]{1,0:T(8,128)(2,1)S(1)} %slice.231), channel_id=1, source_target_pairs={{0,3},{1,0},{2,1},{3,2},{4,7},{5,4},{6,5},{7,6},{8,11},{9,8},{10,9... | collective-permute-start | bytes 1769480 | tf_op jit(solution)/shard_map/ppermute | solution.py:17
  124.5 2.6 collective-permute-start.18
  128.0 2.6 copy.16
  132.4 2.6 slice.232
  136.8 3.7 %fusion = f32[2048,256]{1,0:T(8,128)S(1)} fusion(bf16[2048,1024]{1,0:T(8,128)(2,1)S(1)} %bitcast.25, bf16[2048,1024]{1,0:T(8,128)(2,1)S(1)} %slice.232, bf16[2048,128]{1,0:T(8,128)(2,1)} %collective-permute-done.17, bf16[2048,128]{1,0:T(8,128)(2,1)} %bitcast.4), kind=kOutput, calls=%fused_computation.2 | convolution fusion | flops 2166358016 | bytes 11534336 | tf_op jit(solution)/shard_map/dot_general | solution.py:83
  140.5 2.4 fusion.1
  143.0 2.8 convolution_convert_fusion
  146.8 5.1 %collective-permute-start.31 = (bf16[256,1024]{1,0:T(8,128)(2,1)S(1)}, bf16[256,1024]{1,0:T(8,128)(2,1)S(1)}, u32[]{:S(2)}, u32[]{:S(2)}) collective-permute-start(bf16[256,1024]{1,0:T(8,128)(2,1)S(1)} %bitcast.30), channel_id=1, source_target_pairs={{0,256},{256,4},{4,260},{260,0},{1,257},{257,5},{5,261},{261,1},{2... | collective-permute-start | bytes 1572872 | tf_op jit(solution)/shard_map/ppermute | solution.py:17
  153.8 3.9 %collective-permute-start.35 = (bf16[256,1024]{1,0:T(8,128)(2,1)S(1)}, bf16[256,1024]{1,0:T(8,128)(2,1)S(1)}, u32[]{:S(2)}, u32[]{:S(2)}) collective-permute-start(bf16[256,1024]{1,0:T(8,128)(2,1)S(1)} %bitcast.29), channel_id=1, source_target_pairs={{0,260},{256,0},{4,256},{260,4},{1,261},{257,1},{5,257},{261,5},{2... | collective-permute-start | bytes 1572872 | tf_op jit(solution)/shard_map/ppermute | solution.py:17
  159.9 3.5 %collective-permute-start.23 = (bf16[256,1024]{1,0:T(8,128)(2,1)S(1)}, bf16[256,1024]{1,0:T(8,128)(2,1)S(1)}, u32[]{:S(2)}, u32[]{:S(2)}) collective-permute-start(bf16[256,1024]{1,0:T(8,128)(2,1)S(1)} %get-tuple-element.8), channel_id=1, source_target_pairs={{0,3},{1,0},{2,1},{3,2},{4,7},{5,4},{6,5},{7,6},{8,11},{9,8},{10,9... | collective-permute-start | bytes 1572872 | tf_op jit(solution)/shard_map/ppermute | solution.py:17
  166.3 5.4 %collective-permute-done.35 = bf16[256,1024]{1,0:T(8,128)(2,1)S(1)} collective-permute-done((bf16[256,1024]{1,0:T(8,128)(2,1)S(1)}, bf16[256,1024]{1,0:T(8,128)(2,1)S(1)}, u32[]{:S(2)}, u32[]{:S(2)}) %collective-permute-start.35) | collective-permute-done | bytes 524320 | tf_op jit(solution)/shard_map/ppermute | solution.py:17
  174.8 3.0 collective-permute-start.36
  181.6 5.1 %collective-permute-start.22 = (bf16[256,1024]{1,0:T(8,128)(2,1)S(1)}, bf16[256,1024]{1,0:T(8,128)(2,1)S(1)}, u32[]{:S(2)}, u32[]{:S(2)}) collective-permute-start(bf16[256,1024]{1,0:T(8,128)(2,1)S(1)} %get-tuple-element.7), channel_id=1, source_target_pairs={{0,3},{1,0},{2,1},{3,2},{4,7},{5,4},{6,5},{7,6},{8,11},{9,8},{10,9... | collective-permute-start | bytes 1572872 | tf_op jit(solution)/shard_map/ppermute | solution.py:17
  188.7 5.1 %collective-permute-start.24 = (bf16[256,1024]{1,0:T(8,128)(2,1)S(1)}, bf16[256,1024]{1,0:T(8,128)(2,1)S(1)}, u32[]{:S(2)}, u32[]{:S(2)}) collective-permute-start(bf16[256,1024]{1,0:T(8,128)(2,1)S(1)} %get-tuple-element.11), channel_id=1, source_target_pairs={{0,3},{1,0},{2,1},{3,2},{4,7},{5,4},{6,5},{7,6},{8,11},{9,8},{10,9... | collective-permute-start | bytes 1572872 | tf_op jit(solution)/shard_map/ppermute | solution.py:17
  197.2 4.5 %collective-permute-start.41 = (bf16[64,1024]{1,0:T(8,128)(2,1)S(1)}, bf16[64,1024]{1,0:T(8,128)(2,1)S(1)}, u32[]{:S(2)}, u32[]{:S(2)}) collective-permute-start(bf16[64,1024]{1,0:T(8,128)(2,1)S(1)} %get-tuple-element.26), channel_id=1, source_target_pairs={{0,3},{1,0},{2,1},{3,2},{4,7},{5,4},{6,5},{7,6},{8,11},{9,8},{10,9... | collective-permute-start | bytes 393224 | tf_op jit(solution)/shard_map/ppermute | solution.py:17
  203.6 3.9 %collective-permute-done.20 = bf16[256,1024]{1,0:T(8,128)(2,1)S(1)} collective-permute-done((bf16[256,1024]{1,0:T(8,128)(2,1)S(1)}, bf16[256,1024]{1,0:T(8,128)(2,1)S(1)}, u32[]{:S(2)}, u32[]{:S(2)}) %collective-permute-start.20) | collective-permute-done | bytes 524320 | tf_op jit(solution)/shard_map/ppermute | solution.py:17
  210.3 5.6 %collective-permute-start.27 = (bf16[64,1024]{1,0:T(8,128)(2,1)S(1)}, bf16[64,1024]{1,0:T(8,128)(2,1)S(1)}, u32[]{:S(2)}, u32[]{:S(2)}) collective-permute-start(bf16[64,1024]{1,0:T(8,128)(2,1)S(1)} %get-tuple-element.21), channel_id=1, source_target_pairs={{0,256},{256,4},{4,260},{260,0},{1,257},{257,5},{5,261},{261,1},{2... | collective-permute-start | bytes 393224 | tf_op jit(solution)/shard_map/ppermute | solution.py:17
  217.8 5.1 %collective-permute-start.25 = (bf16[64,1024]{1,0:T(8,128)(2,1)S(1)}, bf16[64,1024]{1,0:T(8,128)(2,1)S(1)}, u32[]{:S(2)}, u32[]{:S(2)}) collective-permute-start(bf16[64,1024]{1,0:T(8,128)(2,1)S(1)} %get-tuple-element.22), channel_id=1, source_target_pairs={{0,256},{256,4},{4,260},{260,0},{1,257},{257,5},{5,261},{261,1},{2... | collective-permute-start | bytes 393224 | tf_op jit(solution)/shard_map/ppermute | solution.py:17
  224.0 3.9 %collective-permute-start.38 = (bf16[64,1024]{1,0:T(8,128)(2,1)S(1)}, bf16[64,1024]{1,0:T(8,128)(2,1)S(1)}, u32[]{:S(2)}, u32[]{:S(2)}) collective-permute-start(bf16[64,1024]{1,0:T(8,128)(2,1)S(1)} %get-tuple-element.30), channel_id=1, source_target_pairs={{0,1},{1,2},{2,3},{3,0},{4,5},{5,6},{6,7},{7,4},{8,9},{9,10},{10,1... | collective-permute-start | bytes 393224 | tf_op jit(solution)/shard_map/ppermute | solution.py:17
  227.9 3.3 %collective-permute-start.42 = (bf16[64,1024]{1,0:T(8,128)(2,1)S(1)}, bf16[64,1024]{1,0:T(8,128)(2,1)S(1)}, u32[]{:S(2)}, u32[]{:S(2)}) collective-permute-start(bf16[64,1024]{1,0:T(8,128)(2,1)S(1)} %get-tuple-element.29), channel_id=1, source_target_pairs={{0,3},{1,0},{2,1},{3,2},{4,7},{5,4},{6,5},{7,6},{8,11},{9,8},{10,9... | collective-permute-start | bytes 393224 | tf_op jit(solution)/shard_map/ppermute | solution.py:17
  233.2 5.1 %collective-permute-start.26 = (bf16[64,1024]{1,0:T(8,128)(2,1)S(1)}, bf16[64,1024]{1,0:T(8,128)(2,1)S(1)}, u32[]{:S(2)}, u32[]{:S(2)}) collective-permute-start(bf16[64,1024]{1,0:T(8,128)(2,1)S(1)} %get-tuple-element.24), channel_id=1, source_target_pairs={{0,256},{256,4},{4,260},{260,0},{1,257},{257,5},{5,261},{261,1},{2... | collective-permute-start | bytes 393224 | tf_op jit(solution)/shard_map/ppermute | solution.py:17
  240.8 5.6 %collective-permute-done.30 = bf16[64,1024]{1,0:T(8,128)(2,1)S(1)} collective-permute-done((bf16[64,1024]{1,0:T(8,128)(2,1)S(1)}, bf16[64,1024]{1,0:T(8,128)(2,1)S(1)}, u32[]{:S(2)}, u32[]{:S(2)}) %collective-permute-start.30) | collective-permute-done | bytes 131104 | tf_op jit(solution)/shard_map/ppermute | solution.py:17
  247.6 66.2 %reduce-scatter.2.cloned.1.call-done = f32[8,2048]{1,0:T(8,128)} async-done(((f32[128,2048]{1,0:T(8,128)}), f32[8,2048]{1,0:T(8,128)}) %reduce-scatter.2.cloned.1.call-update) | async-done | bytes 65552 | tf_op jit(solution)/shard_map/reduce_scatter | solution.py:90
  (125 shorter events, 78.6 us)
Async XLA Ops:
  6.5 307.3 %reduce-scatter.2.cloned.1.call-start = ((), (), s32[]{:S(2)}) async-start(), calls=%async_computation.1 | async-start | bytes 1114112 | tf_op jit(solution)/shard_map/reduce_scatter | solution.py:90
  59.3 16.0 %collective-permute-start.1 = (bf16[128,1152]{1,0:T(8,128)(2,1)S(1)}, bf16[128,1152]{1,0:T(8,128)(2,1)S(1)}, u32[]{:S(2)}, u32[]{:S(2)}) collective-permute-start(bf16[128,1152]{1,0:T(8,128)(2,1)S(1)} %get-tuple-element.33), channel_id=1, source_target_pairs={{0,260},{256,0},{4,256},{260,4},{1,261},{257,1},{5,257},{261,5},{2... | collective-permute-start | bytes 884744 | tf_op jit(solution)/shard_map/ppermute | solution.py:17
  62.8 16.5 %collective-permute-start.10 = (bf16[64,1024]{1,0:T(8,128)(2,1)S(1)}, bf16[64,1024]{1,0:T(8,128)(2,1)S(1)}, u32[]{:S(2)}, u32[]{:S(2)}) collective-permute-start(bf16[64,1024]{1,0:T(8,128)(2,1)S(1)} %slice.234), channel_id=1, source_target_pairs={{0,1},{1,2},{2,3},{3,0},{4,5},{5,6},{6,7},{7,4},{8,9},{9,10},{10,1... | collective-permute-start | bytes 393224 | tf_op jit(solution)/shard_map/ppermute | solution.py:17
  65.1 14.9 %collective-permute-start.11 = (bf16[64,1024]{1,0:T(8,128)(2,1)S(1)}, bf16[64,1024]{1,0:T(8,128)(2,1)S(1)}, u32[]{:S(2)}, u32[]{:S(2)}) collective-permute-start(bf16[64,1024]{1,0:T(8,128)(2,1)S(1)} %slice.235), channel_id=1, source_target_pairs={{0,3},{1,0},{2,1},{3,2},{4,7},{5,4},{6,5},{7,6},{8,11},{9,8},{10,9... | collective-permute-start | bytes 393224 | tf_op jit(solution)/shard_map/ppermute | solution.py:17
  71.7 15.9 %collective-permute-start.2 = (bf16[64,1152]{1,0:T(8,128)(2,1)S(1)}, bf16[64,1152]{1,0:T(8,128)(2,1)S(1)}, u32[]{:S(2)}, u32[]{:S(2)}) collective-permute-start(bf16[64,1152]{1,0:T(8,128)(2,1)S(1)} %slice.228), channel_id=1, source_target_pairs={{0,256},{256,4},{4,260},{260,0},{1,257},{257,5},{5,261},{261,1},{2... | collective-permute-start | bytes 442376 | tf_op jit(solution)/shard_map/ppermute | solution.py:17
  80.8 19.4 %collective-permute-start.12 = (bf16[512,1024]{1,0:T(8,128)(2,1)}, bf16[512,1024]{1,0:T(8,128)(2,1)S(1)}, u32[]{:S(2)}, u32[]{:S(2)}) collective-permute-start(bf16[512,1024]{1,0:T(8,128)(2,1)} %get-tuple-element.49), channel_id=1, source_target_pairs={{0,256},{256,4},{4,260},{260,0},{1,257},{257,5},{5,261},{261,1},{2... | collective-permute-start | bytes 3145736 | tf_op jit(solution)/shard_map/ppermute | solution.py:17
  85.6 20.1 %collective-permute-start.13 = (bf16[512,1024]{1,0:T(8,128)(2,1)}, bf16[512,1024]{1,0:T(8,128)(2,1)}, u32[]{:S(2)}, u32[]{:S(2)}) collective-permute-start(bf16[512,1024]{1,0:T(8,128)(2,1)} %get-tuple-element.49), channel_id=1, source_target_pairs={{0,260},{256,0},{4,256},{260,4},{1,261},{257,1},{5,257},{261,5},{2... | collective-permute-start | bytes 3145736 | tf_op jit(solution)/shard_map/ppermute | solution.py:17
  89.0 23.1 %collective-permute-start.4 = (bf16[512,1152]{1,0:T(8,128)(2,1)}, bf16[512,1152]{1,0:T(8,128)(2,1)S(1)}, u32[]{:S(2)}, u32[]{:S(2)}) collective-permute-start(bf16[512,1152]{1,0:T(8,128)(2,1)} %get-tuple-element.45), channel_id=1, source_target_pairs={{0,1},{1,2},{2,3},{3,0},{4,5},{5,6},{6,7},{7,4},{8,9},{9,10},{10,1... | collective-permute-start | bytes 3538952 | tf_op jit(solution)/shard_map/ppermute | solution.py:17
  90.9 23.3 %collective-permute-start.5 = (bf16[512,1152]{1,0:T(8,128)(2,1)}, bf16[512,1152]{1,0:T(8,128)(2,1)S(1)}, u32[]{:S(2)}, u32[]{:S(2)}) collective-permute-start(bf16[512,1152]{1,0:T(8,128)(2,1)} %get-tuple-element.45), channel_id=1, source_target_pairs={{0,3},{1,0},{2,1},{3,2},{4,7},{5,4},{6,5},{7,6},{8,11},{9,8},{10,9... | collective-permute-start | bytes 3538952 | tf_op jit(solution)/shard_map/ppermute | solution.py:17
  96.1 40.7 %collective-permute-start.17 = (bf16[2048,128]{1,0:T(8,128)(2,1)}, bf16[2048,128]{1,0:T(8,128)(2,1)}, u32[]{:S(2)}, u32[]{:S(2)}) collective-permute-start(bf16[2048,128]{1,0:T(8,128)(2,1)} %bitcast.4), channel_id=1, source_target_pairs={{0,8},{8,0},{1,9},{9,1},{2,10},{10,2},{3,11},{11,3},{4,12},{12,4},... | collective-permute-start | bytes 1572872 | tf_op jit(solution)/shard_map/ppermute | solution.py:73
  100.2 21.5 %collective-permute-start.14 = (bf16[256,1024]{1,0:T(8,128)(2,1)S(1)}, bf16[256,1024]{1,0:T(8,128)(2,1)S(1)}, u32[]{:S(2)}, u32[]{:S(2)}) collective-permute-start(bf16[256,1024]{1,0:T(8,128)(2,1)S(1)} %slice.236), channel_id=1, source_target_pairs={{0,256},{256,4},{4,260},{260,0},{1,257},{257,5},{5,261},{261,1},{2... | collective-permute-start | bytes 1572872 | tf_op jit(solution)/shard_map/ppermute | solution.py:17
  106.8 17.8 %collective-permute-start.15 = (bf16[256,1024]{1,0:T(8,128)(2,1)S(1)}, bf16[256,1024]{1,0:T(8,128)(2,1)S(1)}, u32[]{:S(2)}, u32[]{:S(2)}) collective-permute-start(bf16[256,1024]{1,0:T(8,128)(2,1)S(1)} %slice.237), channel_id=1, source_target_pairs={{0,260},{256,0},{4,256},{260,4},{1,261},{257,1},{5,257},{261,5},{2... | collective-permute-start | bytes 1572872 | tf_op jit(solution)/shard_map/ppermute | solution.py:17
  112.2 18.4 %collective-permute-start.6 = (bf16[256,1152]{1,0:T(8,128)(2,1)S(1)}, bf16[256,1152]{1,0:T(8,128)(2,1)S(1)}, u32[]{:S(2)}, u32[]{:S(2)}) collective-permute-start(bf16[256,1152]{1,0:T(8,128)(2,1)S(1)} %slice.230), channel_id=1, source_target_pairs={{0,1},{1,2},{2,3},{3,0},{4,5},{5,6},{6,7},{7,4},{8,9},{9,10},{10,1... | collective-permute-start | bytes 1769480 | tf_op jit(solution)/shard_map/ppermute | solution.py:17
  114.3 17.2 %collective-permute-start.7 = (bf16[256,1152]{1,0:T(8,128)(2,1)S(1)}, bf16[256,1152]{1,0:T(8,128)(2,1)S(1)}, u32[]{:S(2)}, u32[]{:S(2)}) collective-permute-start(bf16[256,1152]{1,0:T(8,128)(2,1)S(1)} %slice.231), channel_id=1, source_target_pairs={{0,3},{1,0},{2,1},{3,2},{4,7},{5,4},{6,5},{7,6},{8,11},{9,8},{10,9... | collective-permute-start | bytes 1769480 | tf_op jit(solution)/shard_map/ppermute | solution.py:17
  121.7 18.7 %collective-permute-start.16 = (bf16[2048,128]{1,0:T(8,128)(2,1)S(1)}, bf16[2048,128]{1,0:T(8,128)(2,1)S(1)}, u32[]{:S(2)}, u32[]{:S(2)}) collective-permute-start(bf16[2048,128]{1,0:T(8,128)(2,1)S(1)} %bitcast.31), channel_id=1, source_target_pairs={{0,8},{8,0},{1,9},{9,1},{2,10},{10,2},{3,11},{11,3},{4,12},{12,4},... | collective-permute-start | bytes 1572872 | tf_op jit(solution)/shard_map/ppermute | solution.py:72
  124.5 18.4 %collective-permute-start.18 = (bf16[128,2048]{1,0:T(8,128)(2,1)S(1)}, bf16[128,2048]{1,0:T(8,128)(2,1)S(1)}, u32[]{:S(2)}, u32[]{:S(2)}) collective-permute-start(bf16[128,2048]{1,0:T(8,128)(2,1)S(1)} %bitcast.33), channel_id=1, source_target_pairs={{0,8},{8,0},{1,9},{9,1},{2,10},{10,2},{3,11},{11,3},{4,12},{12,4},... | collective-permute-start | bytes 1572872 | tf_op jit(solution)/shard_map/ppermute | solution.py:74
  146.8 17.4 %collective-permute-start.31 = (bf16[256,1024]{1,0:T(8,128)(2,1)S(1)}, bf16[256,1024]{1,0:T(8,128)(2,1)S(1)}, u32[]{:S(2)}, u32[]{:S(2)}) collective-permute-start(bf16[256,1024]{1,0:T(8,128)(2,1)S(1)} %bitcast.30), channel_id=1, source_target_pairs={{0,256},{256,4},{4,260},{260,0},{1,257},{257,5},{5,261},{261,1},{2... | collective-permute-start | bytes 1572872 | tf_op jit(solution)/shard_map/ppermute | solution.py:17
  151.9 29.7 %collective-permute-start.33 = (bf16[256,1024]{1,0:T(8,128)(2,1)S(1)}, bf16[256,1024]{1,0:T(8,128)(2,1)S(1)}, u32[]{:S(2)}, u32[]{:S(2)}) collective-permute-start(bf16[256,1024]{1,0:T(8,128)(2,1)S(1)} %bitcast.28), channel_id=1, source_target_pairs={{0,256},{256,4},{4,260},{260,0},{1,257},{257,5},{5,261},{261,1},{2... | collective-permute-start | bytes 1572872 | tf_op jit(solution)/shard_map/ppermute | solution.py:17
  153.8 17.9 %collective-permute-start.35 = (bf16[256,1024]{1,0:T(8,128)(2,1)S(1)}, bf16[256,1024]{1,0:T(8,128)(2,1)S(1)}, u32[]{:S(2)}, u32[]{:S(2)}) collective-permute-start(bf16[256,1024]{1,0:T(8,128)(2,1)S(1)} %bitcast.29), channel_id=1, source_target_pairs={{0,260},{256,0},{4,256},{260,4},{1,261},{257,1},{5,257},{261,5},{2... | collective-permute-start | bytes 1572872 | tf_op jit(solution)/shard_map/ppermute | solution.py:17
  157.8 29.0 %collective-permute-start.34 = (bf16[256,1024]{1,0:T(8,128)(2,1)S(1)}, bf16[256,1024]{1,0:T(8,128)(2,1)S(1)}, u32[]{:S(2)}, u32[]{:S(2)}) collective-permute-start(bf16[256,1024]{1,0:T(8,128)(2,1)S(1)} %bitcast.27), channel_id=1, source_target_pairs={{0,260},{256,0},{4,256},{260,4},{1,261},{257,1},{5,257},{261,5},{2... | collective-permute-start | bytes 1572872 | tf_op jit(solution)/shard_map/ppermute | solution.py:17
  164.2 15.1 %collective-permute-start.19 = (bf16[256,1024]{1,0:T(8,128)(2,1)S(1)}, bf16[256,1024]{1,0:T(8,128)(2,1)S(1)}, u32[]{:S(2)}, u32[]{:S(2)}) collective-permute-start(bf16[256,1024]{1,0:T(8,128)(2,1)S(1)} %get-tuple-element.10), channel_id=1, source_target_pairs={{0,1},{1,2},{2,3},{3,0},{4,5},{5,6},{6,7},{7,4},{8,9},{9,10},{10,1... | collective-permute-start | bytes 1572872 | tf_op jit(solution)/shard_map/ppermute | solution.py:17
  171.7 17.0 %collective-permute-start.32 = (bf16[256,1024]{1,0:T(8,128)(2,1)S(1)}, bf16[256,1024]{1,0:T(8,128)(2,1)S(1)}, u32[]{:S(2)}, u32[]{:S(2)}) collective-permute-start(bf16[256,1024]{1,0:T(8,128)(2,1)S(1)} %fusion.14), channel_id=1, source_target_pairs={{0,256},{256,4},{4,260},{260,0},{1,257},{257,5},{5,261},{261,1},{2... | collective-permute-start | bytes 1572872 | tf_op jit(solution)/shard_map/ppermute | solution.py:17
  174.8 19.1 %collective-permute-start.36 = (bf16[256,1024]{1,0:T(8,128)(2,1)S(1)}, bf16[256,1024]{1,0:T(8,128)(2,1)S(1)}, u32[]{:S(2)}, u32[]{:S(2)}) collective-permute-start(bf16[256,1024]{1,0:T(8,128)(2,1)S(1)} %fusion.13), channel_id=1, source_target_pairs={{0,260},{256,0},{4,256},{260,4},{1,261},{257,1},{5,257},{261,5},{2... | collective-permute-start | bytes 1572872 | tf_op jit(solution)/shard_map/ppermute | solution.py:17
  179.3 17.9 %collective-permute-start.21 = (bf16[256,1024]{1,0:T(8,128)(2,1)S(1)}, bf16[256,1024]{1,0:T(8,128)(2,1)S(1)}, u32[]{:S(2)}, u32[]{:S(2)}) collective-permute-start(bf16[256,1024]{1,0:T(8,128)(2,1)S(1)} %get-tuple-element.9), channel_id=1, source_target_pairs={{0,1},{1,2},{2,3},{3,0},{4,5},{5,6},{6,7},{7,4},{8,9},{9,10},{10,1... | collective-permute-start | bytes 1572872 | tf_op jit(solution)/shard_map/ppermute | solution.py:17
  181.6 20.1 %collective-permute-start.22 = (bf16[256,1024]{1,0:T(8,128)(2,1)S(1)}, bf16[256,1024]{1,0:T(8,128)(2,1)S(1)}, u32[]{:S(2)}, u32[]{:S(2)}) collective-permute-start(bf16[256,1024]{1,0:T(8,128)(2,1)S(1)} %get-tuple-element.7), channel_id=1, source_target_pairs={{0,3},{1,0},{2,1},{3,2},{4,7},{5,4},{6,5},{7,6},{8,11},{9,8},{10,9... | collective-permute-start | bytes 1572872 | tf_op jit(solution)/shard_map/ppermute | solution.py:17
  186.8 20.8 %collective-permute-start.20 = (bf16[256,1024]{1,0:T(8,128)(2,1)S(1)}, bf16[256,1024]{1,0:T(8,128)(2,1)S(1)}, u32[]{:S(2)}, u32[]{:S(2)}) collective-permute-start(bf16[256,1024]{1,0:T(8,128)(2,1)S(1)} %get-tuple-element.12), channel_id=1, source_target_pairs={{0,1},{1,2},{2,3},{3,0},{4,5},{5,6},{6,7},{7,4},{8,9},{9,10},{10,1... | collective-permute-start | bytes 1572872 | tf_op jit(solution)/shard_map/ppermute | solution.py:17
  188.7 20.8 %collective-permute-start.24 = (bf16[256,1024]{1,0:T(8,128)(2,1)S(1)}, bf16[256,1024]{1,0:T(8,128)(2,1)S(1)}, u32[]{:S(2)}, u32[]{:S(2)}) collective-permute-start(bf16[256,1024]{1,0:T(8,128)(2,1)S(1)} %get-tuple-element.11), channel_id=1, source_target_pairs={{0,3},{1,0},{2,1},{3,2},{4,7},{5,4},{6,5},{7,6},{8,11},{9,8},{10,9... | collective-permute-start | bytes 1572872 | tf_op jit(solution)/shard_map/ppermute | solution.py:17
  194.6 36.6 %collective-permute-start.39 = (bf16[64,1024]{1,0:T(8,128)(2,1)S(1)}, bf16[64,1024]{1,0:T(8,128)(2,1)S(1)}, u32[]{:S(2)}, u32[]{:S(2)}) collective-permute-start(bf16[64,1024]{1,0:T(8,128)(2,1)S(1)} %get-tuple-element.27), channel_id=1, source_target_pairs={{0,1},{1,2},{2,3},{3,0},{4,5},{5,6},{6,7},{7,4},{8,9},{9,10},{10,1... | collective-permute-start | bytes 393224 | tf_op jit(solution)/shard_map/ppermute | solution.py:17
  197.2 18.7 %collective-permute-start.41 = (bf16[64,1024]{1,0:T(8,128)(2,1)S(1)}, bf16[64,1024]{1,0:T(8,128)(2,1)S(1)}, u32[]{:S(2)}, u32[]{:S(2)}) collective-permute-start(bf16[64,1024]{1,0:T(8,128)(2,1)S(1)} %get-tuple-element.26), channel_id=1, source_target_pairs={{0,3},{1,0},{2,1},{3,2},{4,7},{5,4},{6,5},{7,6},{8,11},{9,8},{10,9... | collective-permute-start | bytes 393224 | tf_op jit(solution)/shard_map/ppermute | solution.py:17
  201.7 16.1 %collective-permute-start.37 = (bf16[64,1024]{1,0:T(8,128)(2,1)S(1)}, bf16[64,1024]{1,0:T(8,128)(2,1)S(1)}, u32[]{:S(2)}, u32[]{:S(2)}) collective-permute-start(bf16[64,1024]{1,0:T(8,128)(2,1)S(1)} %get-tuple-element.28), channel_id=1, source_target_pairs={{0,1},{1,2},{2,3},{3,0},{4,5},{5,6},{6,7},{7,4},{8,9},{9,10},{10,1... | collective-permute-start | bytes 393224 | tf_op jit(solution)/shard_map/ppermute | solution.py:17
  207.6 25.6 %collective-permute-start.40 = (bf16[64,1024]{1,0:T(8,128)(2,1)S(1)}, bf16[64,1024]{1,0:T(8,128)(2,1)S(1)}, u32[]{:S(2)}, u32[]{:S(2)}) collective-permute-start(bf16[64,1024]{1,0:T(8,128)(2,1)S(1)} %get-tuple-element.25), channel_id=1, source_target_pairs={{0,3},{1,0},{2,1},{3,2},{4,7},{5,4},{6,5},{7,6},{8,11},{9,8},{10,9... | collective-permute-start | bytes 393224 | tf_op jit(solution)/shard_map/ppermute | solution.py:17
  210.3 30.1 %collective-permute-start.27 = (bf16[64,1024]{1,0:T(8,128)(2,1)S(1)}, bf16[64,1024]{1,0:T(8,128)(2,1)S(1)}, u32[]{:S(2)}, u32[]{:S(2)}) collective-permute-start(bf16[64,1024]{1,0:T(8,128)(2,1)S(1)} %get-tuple-element.21), channel_id=1, source_target_pairs={{0,256},{256,4},{4,260},{260,0},{1,257},{257,5},{5,261},{261,1},{2... | collective-permute-start | bytes 393224 | tf_op jit(solution)/shard_map/ppermute | solution.py:17
  (16 other events, 269.8 us)
Sparse Core Ops, SparseCore 0:
  247.7 66.0 reduce-scatter.1

commit v3 on v2

--- a/solution.py
+++ b/solution.py
@@ -87,8 +87,10 @@
     sum_a = ring_scatter(ring_scatter(out_a, "y").astype(jnp.bfloat16), X)
     sum_b = ring_scatter(ring_scatter(out_b, X).astype(jnp.bfloat16), "y")
     part = lax.optimization_barrier(jnp.concatenate([sum_a, sum_b], axis=1))
-    total = lax.psum_scatter(part, "z", scatter_dimension=0, tiled=True)
-    return lax.optimization_barrier(total).astype(jnp.bfloat16)
+    n = lax.axis_size("z")
+    block = part.shape[0] // n
+    spread = lax.all_to_all(part.astype(jnp.bfloat16), "z", split_axis=0, concat_axis=0, tiled=True)
+    return jnp.sum(spread.reshape(n, block, width).astype(jnp.float32), axis=0).astype(jnp.bfloat16)
 
 
 def solution(mesh):

time: 324 us -> 270 us (0.83)
  waiting for transfers between devices: 88.6 us -> 21.2 us
  blocking collectives: 38.7 us -> 65.7 us
  between operations: 14.2 us -> 0.8 us
    reduce_scatter x1 -> x0, waiting for transfers between devices: 66.2 us -> none  [local(): total = lax.psum_scatter(part, 'z', scatter_dimension=0, tiled=True)]
    all_to_all x0 -> x1, blocking collectives: none -> 27.1 us  [local(): lax.all_to_all(part.astype(jnp.bfloat16), 'z', split_axis=0, concat_axis=...]
  transfers between devices with their start and end apart: 44 -> 43, of which waited for: 11 -> 10; matrix products, arithmetic and copies ran while one was open for 10% -> 13% of each run, Pallas kernels for 0% -> 0%
where the time goes in v3:
time: 270 us; the launch traced here: 268 us
  starting transfers between devices  138 us (51%)
  blocking collectives  65.7 us (24%)
  local copies, waits for them, and re-layouts  27.4 us (10%)
  waiting for transfers between devices  21.2 us (8%)
  matrix products  9.03 us (3%)
  other arithmetic  6.03 us (2%)
    ppermute x40, starting transfers between devices, step(): lax.ppermute(v, axis, [(place[i], place[(i + by) % 4]) for i in range(4)])  131 us
    all_gather x1, blocking collectives, local(): everyone = lax.all_gather(packed, 'z', axis=0, tiled=True)  38.7 us
    all_to_all x1, blocking collectives, local(): lax.all_to_all(part.astype(jnp.bfloat16), 'z', split_axis=0, concat_axis=...  27.1 us
    ppermute x40, waiting for transfers between devices, step(): lax.ppermute(v, axis, [(place[i], place[(i + by) % 4]) for i in range(4)])  21.1 us
    unnamed x22, local copies, waits for them, and re-layouts  14.2 us
  transfers between devices with their start and end apart: 43, of which 10 were waited for; matrix products, arithmetic and copies ran while one was open for 13% of the time, Pallas kernels for 0%

profile of v3, /device:TPU:6, one launch (start us, length us, event | category | flops | bytes accessed | tf_op | source)
XLA Modules:
  0.0 268.0 jit_solution(2014687247986500527)
XLA Ops:
  2.9 38.7 %all_gather.3 = bf16[128,2176]{1,0:T(8,128)(2,1)S(1)} all-gather(bf16[8,2176]{1,0:T(8,128)(2,1)S(1)} %concatenate.56), channel_id=1, replica_groups=mesh['xl'=2,'z'=16,'core'=2,'xh'=2,'y'=4] {'z'}, dimensions={0}, use_global_device_ids=true | all-gather | bytes 591872 | tf_op jit(solution)/shard_map/all_gather | solution.py:63
  42.5 3.5 %collective-permute-start.8 = (bf16[128,1024]{1,0:T(8,128)(2,1)S(1)}, bf16[128,1024]{1,0:T(8,128)(2,1)S(1)}, u32[]{:S(2)}, u32[]{:S(2)}) collective-permute-start(bf16[128,1024]{1,0:T(8,128)(2,1)S(1)} %get-tuple-element.36), channel_id=1, source_target_pairs={{0,1},{1,2},{2,3},{3,0},{4,5},{5,6},{6,7},{7,4},{8,9},{9,10},{10,1... | collective-permute-start | bytes 786440 | tf_op jit(solution)/shard_map/ppermute | solution.py:17
  45.9 3.6 %collective-permute-start.9 = (bf16[128,1024]{1,0:T(8,128)(2,1)S(1)}, bf16[128,1024]{1,0:T(8,128)(2,1)S(1)}, u32[]{:S(2)}, u32[]{:S(2)}) collective-permute-start(bf16[128,1024]{1,0:T(8,128)(2,1)S(1)} %get-tuple-element.36), channel_id=1, source_target_pairs={{0,3},{1,0},{2,1},{3,2},{4,7},{5,4},{6,5},{7,6},{8,11},{9,8},{10,9... | collective-permute-start | bytes 786440 | tf_op jit(solution)/shard_map/ppermute | solution.py:17
  52.8 3.5 %collective-permute-start.1 = (bf16[128,1152]{1,0:T(8,128)(2,1)S(1)}, bf16[128,1152]{1,0:T(8,128)(2,1)S(1)}, u32[]{:S(2)}, u32[]{:S(2)}) collective-permute-start(bf16[128,1152]{1,0:T(8,128)(2,1)S(1)} %get-tuple-element.33), channel_id=1, source_target_pairs={{0,260},{256,0},{4,256},{260,4},{1,261},{257,1},{5,257},{261,5},{2... | collective-permute-start | bytes 884744 | tf_op jit(solution)/shard_map/ppermute | solution.py:17
  58.6 4.8 %collective-permute-start.11 = (bf16[64,1024]{1,0:T(8,128)(2,1)S(1)}, bf16[64,1024]{1,0:T(8,128)(2,1)S(1)}, u32[]{:S(2)}, u32[]{:S(2)}) collective-permute-start(bf16[64,1024]{1,0:T(8,128)(2,1)S(1)} %slice.235), channel_id=1, source_target_pairs={{0,3},{1,0},{2,1},{3,2},{4,7},{5,4},{6,5},{7,6},{8,11},{9,8},{10,9... | collective-permute-start | bytes 393224 | tf_op jit(solution)/shard_map/ppermute | solution.py:17
  65.2 3.6 %collective-permute-start.2 = (bf16[64,1152]{1,0:T(8,128)(2,1)S(1)}, bf16[64,1152]{1,0:T(8,128)(2,1)S(1)}, u32[]{:S(2)}, u32[]{:S(2)}) collective-permute-start(bf16[64,1152]{1,0:T(8,128)(2,1)S(1)} %slice.228), channel_id=1, source_target_pairs={{0,256},{256,4},{4,260},{260,0},{1,257},{257,5},{5,261},{261,1},{2... | collective-permute-start | bytes 442376 | tf_op jit(solution)/shard_map/ppermute | solution.py:17
  74.3 4.8 %collective-permute-start.12 = (bf16[512,1024]{1,0:T(8,128)(2,1)}, bf16[512,1024]{1,0:T(8,128)(2,1)S(1)}, u32[]{:S(2)}, u32[]{:S(2)}) collective-permute-start(bf16[512,1024]{1,0:T(8,128)(2,1)} %get-tuple-element.49), channel_id=1, source_target_pairs={{0,256},{256,4},{4,260},{260,0},{1,257},{257,5},{5,261},{261,1},{2... | collective-permute-start | bytes 3145736 | tf_op jit(solution)/shard_map/ppermute | solution.py:17
  84.4 5.1 %collective-permute-start.5 = (bf16[512,1152]{1,0:T(8,128)(2,1)}, bf16[512,1152]{1,0:T(8,128)(2,1)S(1)}, u32[]{:S(2)}, u32[]{:S(2)}) collective-permute-start(bf16[512,1152]{1,0:T(8,128)(2,1)} %get-tuple-element.45), channel_id=1, source_target_pairs={{0,3},{1,0},{2,1},{3,2},{4,7},{5,4},{6,5},{7,6},{8,11},{9,8},{10,9... | collective-permute-start | bytes 3538952 | tf_op jit(solution)/shard_map/ppermute | solution.py:17
  93.7 5.5 %collective-permute-start.14 = (bf16[256,1024]{1,0:T(8,128)(2,1)S(1)}, bf16[256,1024]{1,0:T(8,128)(2,1)S(1)}, u32[]{:S(2)}, u32[]{:S(2)}) collective-permute-start(bf16[256,1024]{1,0:T(8,128)(2,1)S(1)} %slice.236), channel_id=1, source_target_pairs={{0,256},{256,4},{4,260},{260,0},{1,257},{257,5},{5,261},{261,1},{2... | collective-permute-start | bytes 1572872 | tf_op jit(solution)/shard_map/ppermute | solution.py:17
  107.8 5.1 %collective-permute-start.7 = (bf16[256,1152]{1,0:T(8,128)(2,1)S(1)}, bf16[256,1152]{1,0:T(8,128)(2,1)S(1)}, u32[]{:S(2)}, u32[]{:S(2)}) collective-permute-start(bf16[256,1152]{1,0:T(8,128)(2,1)S(1)} %slice.231), channel_id=1, source_target_pairs={{0,3},{1,0},{2,1},{3,2},{4,7},{5,4},{6,5},{7,6},{8,11},{9,8},{10,9... | collective-permute-start | bytes 1769480 | tf_op jit(solution)/shard_map/ppermute | solution.py:17
  118.0 2.6 collective-permute-start.18
  121.5 2.6 copy.16
  125.8 2.6 slice.232
  130.3 3.7 %fusion = f32[2048,256]{1,0:T(8,128)S(1)} fusion(bf16[2048,1024]{1,0:T(8,128)(2,1)S(1)} %bitcast.28, bf16[2048,1024]{1,0:T(8,128)(2,1)S(1)} %slice.232, bf16[2048,128]{1,0:T(8,128)(2,1)} %collective-permute-done.17, bf16[2048,128]{1,0:T(8,128)(2,1)} %bitcast.4), kind=kOutput, calls=%fused_computation.2 | convolution fusion | flops 2166358016 | bytes 11534336 | tf_op jit(solution)/shard_map/dot_general | solution.py:83
  134.0 2.5 fusion.1
  136.5 2.9 %convolution_convert_fusion = bf16[2048,2048]{1,0:T(8,128)(2,1)S(1)} fusion(f32[2048,256]{1,0:T(8,128)S(1)} %fusion, f32[2048,256]{1,0:T(8,128)S(1)} %fusion.1, bf16[128,2048]{1,0:T(8,128)(2,1)S(1)} %collective-permute-done.18, bf16[128,2048]{1,0:T(8,128)(2,1)S(1)} %bitcast.38, f32[2048]{0:T(1024)S(1)} %get-tuple-element.6, f32[2048]{0:T(1024)S(1)} %get-tuple-element.5, ...), kind=kOutput, calls=%fused_computation.1 | convolution fusion | flops 2157969408 | bytes 13648128 | tf_op jit(solution)/shard_map/dot_general | solution.py:85
  140.4 5.1 %collective-permute-start.31 = (bf16[256,1024]{1,0:T(8,128)(2,1)S(1)}, bf16[256,1024]{1,0:T(8,128)(2,1)S(1)}, u32[]{:S(2)}, u32[]{:S(2)}) collective-permute-start(bf16[256,1024]{1,0:T(8,128)(2,1)S(1)} %bitcast.34), channel_id=1, source_target_pairs={{0,256},{256,4},{4,260},{260,0},{1,257},{257,5},{5,261},{261,1},{2... | collective-permute-start | bytes 1572872 | tf_op jit(solution)/shard_map/ppermute | solution.py:17
  147.4 3.9 %collective-permute-start.35 = (bf16[256,1024]{1,0:T(8,128)(2,1)S(1)}, bf16[256,1024]{1,0:T(8,128)(2,1)S(1)}, u32[]{:S(2)}, u32[]{:S(2)}) collective-permute-start(bf16[256,1024]{1,0:T(8,128)(2,1)S(1)} %bitcast.33), channel_id=1, source_target_pairs={{0,260},{256,0},{4,256},{260,4},{1,261},{257,1},{5,257},{261,5},{2... | collective-permute-start | bytes 1572872 | tf_op jit(solution)/shard_map/ppermute | solution.py:17
  153.5 3.5 %collective-permute-start.23 = (bf16[256,1024]{1,0:T(8,128)(2,1)S(1)}, bf16[256,1024]{1,0:T(8,128)(2,1)S(1)}, u32[]{:S(2)}, u32[]{:S(2)}) collective-permute-start(bf16[256,1024]{1,0:T(8,128)(2,1)S(1)} %get-tuple-element.8), channel_id=1, source_target_pairs={{0,3},{1,0},{2,1},{3,2},{4,7},{5,4},{6,5},{7,6},{8,11},{9,8},{10,9... | collective-permute-start | bytes 1572872 | tf_op jit(solution)/shard_map/ppermute | solution.py:17
  159.9 5.4 %collective-permute-done.35 = bf16[256,1024]{1,0:T(8,128)(2,1)S(1)} collective-permute-done((bf16[256,1024]{1,0:T(8,128)(2,1)S(1)}, bf16[256,1024]{1,0:T(8,128)(2,1)S(1)}, u32[]{:S(2)}, u32[]{:S(2)}) %collective-permute-start.35) | collective-permute-done | bytes 524320 | tf_op jit(solution)/shard_map/ppermute | solution.py:17
  168.4 3.0 %collective-permute-start.36 = (bf16[256,1024]{1,0:T(8,128)(2,1)S(1)}, bf16[256,1024]{1,0:T(8,128)(2,1)S(1)}, u32[]{:S(2)}, u32[]{:S(2)}) collective-permute-start(bf16[256,1024]{1,0:T(8,128)(2,1)S(1)} %fusion.13), channel_id=1, source_target_pairs={{0,260},{256,0},{4,256},{260,4},{1,261},{257,1},{5,257},{261,5},{2... | collective-permute-start | bytes 1572872 | tf_op jit(solution)/shard_map/ppermute | solution.py:17
  175.3 5.1 %collective-permute-start.22 = (bf16[256,1024]{1,0:T(8,128)(2,1)S(1)}, bf16[256,1024]{1,0:T(8,128)(2,1)S(1)}, u32[]{:S(2)}, u32[]{:S(2)}) collective-permute-start(bf16[256,1024]{1,0:T(8,128)(2,1)S(1)} %get-tuple-element.7), channel_id=1, source_target_pairs={{0,3},{1,0},{2,1},{3,2},{4,7},{5,4},{6,5},{7,6},{8,11},{9,8},{10,9... | collective-permute-start | bytes 1572872 | tf_op jit(solution)/shard_map/ppermute | solution.py:17
  182.3 5.1 %collective-permute-start.24 = (bf16[256,1024]{1,0:T(8,128)(2,1)S(1)}, bf16[256,1024]{1,0:T(8,128)(2,1)S(1)}, u32[]{:S(2)}, u32[]{:S(2)}) collective-permute-start(bf16[256,1024]{1,0:T(8,128)(2,1)S(1)} %get-tuple-element.11), channel_id=1, source_target_pairs={{0,3},{1,0},{2,1},{3,2},{4,7},{5,4},{6,5},{7,6},{8,11},{9,8},{10,9... | collective-permute-start | bytes 1572872 | tf_op jit(solution)/shard_map/ppermute | solution.py:17
  190.8 4.9 %collective-permute-start.41 = (bf16[64,1024]{1,0:T(8,128)(2,1)S(1)}, bf16[64,1024]{1,0:T(8,128)(2,1)S(1)}, u32[]{:S(2)}, u32[]{:S(2)}) collective-permute-start(bf16[64,1024]{1,0:T(8,128)(2,1)S(1)} %get-tuple-element.26), channel_id=1, source_target_pairs={{0,3},{1,0},{2,1},{3,2},{4,7},{5,4},{6,5},{7,6},{8,11},{9,8},{10,9... | collective-permute-start | bytes 393224 | tf_op jit(solution)/shard_map/ppermute | solution.py:17
  197.7 3.2 %collective-permute-done.20 = bf16[256,1024]{1,0:T(8,128)(2,1)S(1)} collective-permute-done((bf16[256,1024]{1,0:T(8,128)(2,1)S(1)}, bf16[256,1024]{1,0:T(8,128)(2,1)S(1)}, u32[]{:S(2)}, u32[]{:S(2)}) %collective-permute-start.20) | collective-permute-done | bytes 524320 | tf_op jit(solution)/shard_map/ppermute | solution.py:17
  203.6 5.9 %collective-permute-start.27 = (bf16[64,1024]{1,0:T(8,128)(2,1)S(1)}, bf16[64,1024]{1,0:T(8,128)(2,1)S(1)}, u32[]{:S(2)}, u32[]{:S(2)}) collective-permute-start(bf16[64,1024]{1,0:T(8,128)(2,1)S(1)} %get-tuple-element.21), channel_id=1, source_target_pairs={{0,256},{256,4},{4,260},{260,0},{1,257},{257,5},{5,261},{261,1},{2... | collective-permute-start | bytes 393224 | tf_op jit(solution)/shard_map/ppermute | solution.py:17
  211.5 5.1 %collective-permute-start.25 = (bf16[64,1024]{1,0:T(8,128)(2,1)S(1)}, bf16[64,1024]{1,0:T(8,128)(2,1)S(1)}, u32[]{:S(2)}, u32[]{:S(2)}) collective-permute-start(bf16[64,1024]{1,0:T(8,128)(2,1)S(1)} %get-tuple-element.22), channel_id=1, source_target_pairs={{0,256},{256,4},{4,260},{260,0},{1,257},{257,5},{5,261},{261,1},{2... | collective-permute-start | bytes 393224 | tf_op jit(solution)/shard_map/ppermute | solution.py:17
  217.6 3.9 %collective-permute-start.38 = (bf16[64,1024]{1,0:T(8,128)(2,1)S(1)}, bf16[64,1024]{1,0:T(8,128)(2,1)S(1)}, u32[]{:S(2)}, u32[]{:S(2)}) collective-permute-start(bf16[64,1024]{1,0:T(8,128)(2,1)S(1)} %get-tuple-element.30), channel_id=1, source_target_pairs={{0,1},{1,2},{2,3},{3,0},{4,5},{5,6},{6,7},{7,4},{8,9},{9,10},{10,1... | collective-permute-start | bytes 393224 | tf_op jit(solution)/shard_map/ppermute | solution.py:17
  221.6 3.3 %collective-permute-start.42 = (bf16[64,1024]{1,0:T(8,128)(2,1)S(1)}, bf16[64,1024]{1,0:T(8,128)(2,1)S(1)}, u32[]{:S(2)}, u32[]{:S(2)}) collective-permute-start(bf16[64,1024]{1,0:T(8,128)(2,1)S(1)} %get-tuple-element.29), channel_id=1, source_target_pairs={{0,3},{1,0},{2,1},{3,2},{4,7},{5,4},{6,5},{7,6},{8,11},{9,8},{10,9... | collective-permute-start | bytes 393224 | tf_op jit(solution)/shard_map/ppermute | solution.py:17
  226.9 5.1 %collective-permute-start.26 = (bf16[64,1024]{1,0:T(8,128)(2,1)S(1)}, bf16[64,1024]{1,0:T(8,128)(2,1)S(1)}, u32[]{:S(2)}, u32[]{:S(2)}) collective-permute-start(bf16[64,1024]{1,0:T(8,128)(2,1)S(1)} %get-tuple-element.24), channel_id=1, source_target_pairs={{0,256},{256,4},{4,260},{260,0},{1,257},{257,5},{5,261},{261,1},{2... | collective-permute-start | bytes 393224 | tf_op jit(solution)/shard_map/ppermute | solution.py:17
  234.5 5.6 %collective-permute-done.30 = bf16[64,1024]{1,0:T(8,128)(2,1)S(1)} collective-permute-done((bf16[64,1024]{1,0:T(8,128)(2,1)S(1)}, bf16[64,1024]{1,0:T(8,128)(2,1)S(1)}, u32[]{:S(2)}, u32[]{:S(2)}) %collective-permute-start.30) | collective-permute-done | bytes 131104 | tf_op jit(solution)/shard_map/ppermute | solution.py:17
  240.3 27.1 %all_to_all.9 = bf16[16,8,2048]{2,1,0:T(8,128)(2,1)S(1)} all-to-all(bf16[16,8,2048]{2,1,0:T(8,128)(2,1)S(1)} %bitcast.30), channel_id=1, replica_groups=mesh['xl'=2,'z'=16,'core'=2,'xh'=2,'y'=4] {'z'}, dimensions={0} | all-to-all | bytes 1048576 | tf_op jit(solution)/shard_map/all_to_all | solution.py:92
  (123 shorter events, 76.9 us)
Async XLA Ops:
  52.8 16.0 %collective-permute-start.1 = (bf16[128,1152]{1,0:T(8,128)(2,1)S(1)}, bf16[128,1152]{1,0:T(8,128)(2,1)S(1)}, u32[]{:S(2)}, u32[]{:S(2)}) collective-permute-start(bf16[128,1152]{1,0:T(8,128)(2,1)S(1)} %get-tuple-element.33), channel_id=1, source_target_pairs={{0,260},{256,0},{4,256},{260,4},{1,261},{257,1},{5,257},{261,5},{2... | collective-permute-start | bytes 884744 | tf_op jit(solution)/shard_map/ppermute | solution.py:17
  56.3 16.5 %collective-permute-start.10 = (bf16[64,1024]{1,0:T(8,128)(2,1)S(1)}, bf16[64,1024]{1,0:T(8,128)(2,1)S(1)}, u32[]{:S(2)}, u32[]{:S(2)}) collective-permute-start(bf16[64,1024]{1,0:T(8,128)(2,1)S(1)} %slice.234), channel_id=1, source_target_pairs={{0,1},{1,2},{2,3},{3,0},{4,5},{5,6},{6,7},{7,4},{8,9},{9,10},{10,1... | collective-permute-start | bytes 393224 | tf_op jit(solution)/shard_map/ppermute | solution.py:17
  58.6 14.9 %collective-permute-start.11 = (bf16[64,1024]{1,0:T(8,128)(2,1)S(1)}, bf16[64,1024]{1,0:T(8,128)(2,1)S(1)}, u32[]{:S(2)}, u32[]{:S(2)}) collective-permute-start(bf16[64,1024]{1,0:T(8,128)(2,1)S(1)} %slice.235), channel_id=1, source_target_pairs={{0,3},{1,0},{2,1},{3,2},{4,7},{5,4},{6,5},{7,6},{8,11},{9,8},{10,9... | collective-permute-start | bytes 393224 | tf_op jit(solution)/shard_map/ppermute | solution.py:17
  65.2 15.8 %collective-permute-start.2 = (bf16[64,1152]{1,0:T(8,128)(2,1)S(1)}, bf16[64,1152]{1,0:T(8,128)(2,1)S(1)}, u32[]{:S(2)}, u32[]{:S(2)}) collective-permute-start(bf16[64,1152]{1,0:T(8,128)(2,1)S(1)} %slice.228), channel_id=1, source_target_pairs={{0,256},{256,4},{4,260},{260,0},{1,257},{257,5},{5,261},{261,1},{2... | collective-permute-start | bytes 442376 | tf_op jit(solution)/shard_map/ppermute | solution.py:17
  74.3 19.4 %collective-permute-start.12 = (bf16[512,1024]{1,0:T(8,128)(2,1)}, bf16[512,1024]{1,0:T(8,128)(2,1)S(1)}, u32[]{:S(2)}, u32[]{:S(2)}) collective-permute-start(bf16[512,1024]{1,0:T(8,128)(2,1)} %get-tuple-element.49), channel_id=1, source_target_pairs={{0,256},{256,4},{4,260},{260,0},{1,257},{257,5},{5,261},{261,1},{2... | collective-permute-start | bytes 3145736 | tf_op jit(solution)/shard_map/ppermute | solution.py:17
  79.1 20.1 %collective-permute-start.13 = (bf16[512,1024]{1,0:T(8,128)(2,1)}, bf16[512,1024]{1,0:T(8,128)(2,1)}, u32[]{:S(2)}, u32[]{:S(2)}) collective-permute-start(bf16[512,1024]{1,0:T(8,128)(2,1)} %get-tuple-element.49), channel_id=1, source_target_pairs={{0,260},{256,0},{4,256},{260,4},{1,261},{257,1},{5,257},{261,5},{2... | collective-permute-start | bytes 3145736 | tf_op jit(solution)/shard_map/ppermute | solution.py:17
  82.5 23.1 %collective-permute-start.4 = (bf16[512,1152]{1,0:T(8,128)(2,1)}, bf16[512,1152]{1,0:T(8,128)(2,1)S(1)}, u32[]{:S(2)}, u32[]{:S(2)}) collective-permute-start(bf16[512,1152]{1,0:T(8,128)(2,1)} %get-tuple-element.45), channel_id=1, source_target_pairs={{0,1},{1,2},{2,3},{3,0},{4,5},{5,6},{6,7},{7,4},{8,9},{9,10},{10,1... | collective-permute-start | bytes 3538952 | tf_op jit(solution)/shard_map/ppermute | solution.py:17
  84.4 23.3 %collective-permute-start.5 = (bf16[512,1152]{1,0:T(8,128)(2,1)}, bf16[512,1152]{1,0:T(8,128)(2,1)S(1)}, u32[]{:S(2)}, u32[]{:S(2)}) collective-permute-start(bf16[512,1152]{1,0:T(8,128)(2,1)} %get-tuple-element.45), channel_id=1, source_target_pairs={{0,3},{1,0},{2,1},{3,2},{4,7},{5,4},{6,5},{7,6},{8,11},{9,8},{10,9... | collective-permute-start | bytes 3538952 | tf_op jit(solution)/shard_map/ppermute | solution.py:17
  89.6 40.7 %collective-permute-start.17 = (bf16[2048,128]{1,0:T(8,128)(2,1)}, bf16[2048,128]{1,0:T(8,128)(2,1)}, u32[]{:S(2)}, u32[]{:S(2)}) collective-permute-start(bf16[2048,128]{1,0:T(8,128)(2,1)} %bitcast.4), channel_id=1, source_target_pairs={{0,8},{8,0},{1,9},{9,1},{2,10},{10,2},{3,11},{11,3},{4,12},{12,4},... | collective-permute-start | bytes 1572872 | tf_op jit(solution)/shard_map/ppermute | solution.py:73
  93.7 21.5 %collective-permute-start.14 = (bf16[256,1024]{1,0:T(8,128)(2,1)S(1)}, bf16[256,1024]{1,0:T(8,128)(2,1)S(1)}, u32[]{:S(2)}, u32[]{:S(2)}) collective-permute-start(bf16[256,1024]{1,0:T(8,128)(2,1)S(1)} %slice.236), channel_id=1, source_target_pairs={{0,256},{256,4},{4,260},{260,0},{1,257},{257,5},{5,261},{261,1},{2... | collective-permute-start | bytes 1572872 | tf_op jit(solution)/shard_map/ppermute | solution.py:17
  100.3 17.7 %collective-permute-start.15 = (bf16[256,1024]{1,0:T(8,128)(2,1)S(1)}, bf16[256,1024]{1,0:T(8,128)(2,1)S(1)}, u32[]{:S(2)}, u32[]{:S(2)}) collective-permute-start(bf16[256,1024]{1,0:T(8,128)(2,1)S(1)} %slice.237), channel_id=1, source_target_pairs={{0,260},{256,0},{4,256},{260,4},{1,261},{257,1},{5,257},{261,5},{2... | collective-permute-start | bytes 1572872 | tf_op jit(solution)/shard_map/ppermute | solution.py:17
  105.7 18.4 %collective-permute-start.6 = (bf16[256,1152]{1,0:T(8,128)(2,1)S(1)}, bf16[256,1152]{1,0:T(8,128)(2,1)S(1)}, u32[]{:S(2)}, u32[]{:S(2)}) collective-permute-start(bf16[256,1152]{1,0:T(8,128)(2,1)S(1)} %slice.230), channel_id=1, source_target_pairs={{0,1},{1,2},{2,3},{3,0},{4,5},{5,6},{6,7},{7,4},{8,9},{9,10},{10,1... | collective-permute-start | bytes 1769480 | tf_op jit(solution)/shard_map/ppermute | solution.py:17
  107.8 17.1 %collective-permute-start.7 = (bf16[256,1152]{1,0:T(8,128)(2,1)S(1)}, bf16[256,1152]{1,0:T(8,128)(2,1)S(1)}, u32[]{:S(2)}, u32[]{:S(2)}) collective-permute-start(bf16[256,1152]{1,0:T(8,128)(2,1)S(1)} %slice.231), channel_id=1, source_target_pairs={{0,3},{1,0},{2,1},{3,2},{4,7},{5,4},{6,5},{7,6},{8,11},{9,8},{10,9... | collective-permute-start | bytes 1769480 | tf_op jit(solution)/shard_map/ppermute | solution.py:17
  115.2 18.8 %collective-permute-start.16 = (bf16[2048,128]{1,0:T(8,128)(2,1)S(1)}, bf16[2048,128]{1,0:T(8,128)(2,1)S(1)}, u32[]{:S(2)}, u32[]{:S(2)}) collective-permute-start(bf16[2048,128]{1,0:T(8,128)(2,1)S(1)} %bitcast.35), channel_id=1, source_target_pairs={{0,8},{8,0},{1,9},{9,1},{2,10},{10,2},{3,11},{11,3},{4,12},{12,4},... | collective-permute-start | bytes 1572872 | tf_op jit(solution)/shard_map/ppermute | solution.py:72
  118.0 18.5 %collective-permute-start.18 = (bf16[128,2048]{1,0:T(8,128)(2,1)S(1)}, bf16[128,2048]{1,0:T(8,128)(2,1)S(1)}, u32[]{:S(2)}, u32[]{:S(2)}) collective-permute-start(bf16[128,2048]{1,0:T(8,128)(2,1)S(1)} %bitcast.37), channel_id=1, source_target_pairs={{0,8},{8,0},{1,9},{9,1},{2,10},{10,2},{3,11},{11,3},{4,12},{12,4},... | collective-permute-start | bytes 1572872 | tf_op jit(solution)/shard_map/ppermute | solution.py:74
  140.4 17.4 %collective-permute-start.31 = (bf16[256,1024]{1,0:T(8,128)(2,1)S(1)}, bf16[256,1024]{1,0:T(8,128)(2,1)S(1)}, u32[]{:S(2)}, u32[]{:S(2)}) collective-permute-start(bf16[256,1024]{1,0:T(8,128)(2,1)S(1)} %bitcast.34), channel_id=1, source_target_pairs={{0,256},{256,4},{4,260},{260,0},{1,257},{257,5},{5,261},{261,1},{2... | collective-permute-start | bytes 1572872 | tf_op jit(solution)/shard_map/ppermute | solution.py:17
  145.5 29.8 %collective-permute-start.33 = (bf16[256,1024]{1,0:T(8,128)(2,1)S(1)}, bf16[256,1024]{1,0:T(8,128)(2,1)S(1)}, u32[]{:S(2)}, u32[]{:S(2)}) collective-permute-start(bf16[256,1024]{1,0:T(8,128)(2,1)S(1)} %bitcast.32), channel_id=1, source_target_pairs={{0,256},{256,4},{4,260},{260,0},{1,257},{257,5},{5,261},{261,1},{2... | collective-permute-start | bytes 1572872 | tf_op jit(solution)/shard_map/ppermute | solution.py:17
  147.4 17.9 %collective-permute-start.35 = (bf16[256,1024]{1,0:T(8,128)(2,1)S(1)}, bf16[256,1024]{1,0:T(8,128)(2,1)S(1)}, u32[]{:S(2)}, u32[]{:S(2)}) collective-permute-start(bf16[256,1024]{1,0:T(8,128)(2,1)S(1)} %bitcast.33), channel_id=1, source_target_pairs={{0,260},{256,0},{4,256},{260,4},{1,261},{257,1},{5,257},{261,5},{2... | collective-permute-start | bytes 1572872 | tf_op jit(solution)/shard_map/ppermute | solution.py:17
  151.3 29.1 %collective-permute-start.34 = (bf16[256,1024]{1,0:T(8,128)(2,1)S(1)}, bf16[256,1024]{1,0:T(8,128)(2,1)S(1)}, u32[]{:S(2)}, u32[]{:S(2)}) collective-permute-start(bf16[256,1024]{1,0:T(8,128)(2,1)S(1)} %bitcast.31), channel_id=1, source_target_pairs={{0,260},{256,0},{4,256},{260,4},{1,261},{257,1},{5,257},{261,5},{2... | collective-permute-start | bytes 1572872 | tf_op jit(solution)/shard_map/ppermute | solution.py:17
  153.5 14.9 %collective-permute-start.23 = (bf16[256,1024]{1,0:T(8,128)(2,1)S(1)}, bf16[256,1024]{1,0:T(8,128)(2,1)S(1)}, u32[]{:S(2)}, u32[]{:S(2)}) collective-permute-start(bf16[256,1024]{1,0:T(8,128)(2,1)S(1)} %get-tuple-element.8), channel_id=1, source_target_pairs={{0,3},{1,0},{2,1},{3,2},{4,7},{5,4},{6,5},{7,6},{8,11},{9,8},{10,9... | collective-permute-start | bytes 1572872 | tf_op jit(solution)/shard_map/ppermute | solution.py:17
  157.8 15.1 %collective-permute-start.19 = (bf16[256,1024]{1,0:T(8,128)(2,1)S(1)}, bf16[256,1024]{1,0:T(8,128)(2,1)S(1)}, u32[]{:S(2)}, u32[]{:S(2)}) collective-permute-start(bf16[256,1024]{1,0:T(8,128)(2,1)S(1)} %get-tuple-element.10), channel_id=1, source_target_pairs={{0,1},{1,2},{2,3},{3,0},{4,5},{5,6},{6,7},{7,4},{8,9},{9,10},{10,1... | collective-permute-start | bytes 1572872 | tf_op jit(solution)/shard_map/ppermute | solution.py:17
  165.3 17.0 %collective-permute-start.32 = (bf16[256,1024]{1,0:T(8,128)(2,1)S(1)}, bf16[256,1024]{1,0:T(8,128)(2,1)S(1)}, u32[]{:S(2)}, u32[]{:S(2)}) collective-permute-start(bf16[256,1024]{1,0:T(8,128)(2,1)S(1)} %fusion.14), channel_id=1, source_target_pairs={{0,256},{256,4},{4,260},{260,0},{1,257},{257,5},{5,261},{261,1},{2... | collective-permute-start | bytes 1572872 | tf_op jit(solution)/shard_map/ppermute | solution.py:17
  168.4 19.1 %collective-permute-start.36 = (bf16[256,1024]{1,0:T(8,128)(2,1)S(1)}, bf16[256,1024]{1,0:T(8,128)(2,1)S(1)}, u32[]{:S(2)}, u32[]{:S(2)}) collective-permute-start(bf16[256,1024]{1,0:T(8,128)(2,1)S(1)} %fusion.13), channel_id=1, source_target_pairs={{0,260},{256,0},{4,256},{260,4},{1,261},{257,1},{5,257},{261,5},{2... | collective-permute-start | bytes 1572872 | tf_op jit(solution)/shard_map/ppermute | solution.py:17
  172.9 17.9 %collective-permute-start.21 = (bf16[256,1024]{1,0:T(8,128)(2,1)S(1)}, bf16[256,1024]{1,0:T(8,128)(2,1)S(1)}, u32[]{:S(2)}, u32[]{:S(2)}) collective-permute-start(bf16[256,1024]{1,0:T(8,128)(2,1)S(1)} %get-tuple-element.9), channel_id=1, source_target_pairs={{0,1},{1,2},{2,3},{3,0},{4,5},{5,6},{6,7},{7,4},{8,9},{9,10},{10,1... | collective-permute-start | bytes 1572872 | tf_op jit(solution)/shard_map/ppermute | solution.py:17
  175.3 20.5 %collective-permute-start.22 = (bf16[256,1024]{1,0:T(8,128)(2,1)S(1)}, bf16[256,1024]{1,0:T(8,128)(2,1)S(1)}, u32[]{:S(2)}, u32[]{:S(2)}) collective-permute-start(bf16[256,1024]{1,0:T(8,128)(2,1)S(1)} %get-tuple-element.7), channel_id=1, source_target_pairs={{0,3},{1,0},{2,1},{3,2},{4,7},{5,4},{6,5},{7,6},{8,11},{9,8},{10,9... | collective-permute-start | bytes 1572872 | tf_op jit(solution)/shard_map/ppermute | solution.py:17
  180.4 20.5 %collective-permute-start.20 = (bf16[256,1024]{1,0:T(8,128)(2,1)S(1)}, bf16[256,1024]{1,0:T(8,128)(2,1)S(1)}, u32[]{:S(2)}, u32[]{:S(2)}) collective-permute-start(bf16[256,1024]{1,0:T(8,128)(2,1)S(1)} %get-tuple-element.12), channel_id=1, source_target_pairs={{0,1},{1,2},{2,3},{3,0},{4,5},{5,6},{6,7},{7,4},{8,9},{9,10},{10,1... | collective-permute-start | bytes 1572872 | tf_op jit(solution)/shard_map/ppermute | solution.py:17
  182.3 20.5 %collective-permute-start.24 = (bf16[256,1024]{1,0:T(8,128)(2,1)S(1)}, bf16[256,1024]{1,0:T(8,128)(2,1)S(1)}, u32[]{:S(2)}, u32[]{:S(2)}) collective-permute-start(bf16[256,1024]{1,0:T(8,128)(2,1)S(1)} %get-tuple-element.11), channel_id=1, source_target_pairs={{0,3},{1,0},{2,1},{3,2},{4,7},{5,4},{6,5},{7,6},{8,11},{9,8},{10,9... | collective-permute-start | bytes 1572872 | tf_op jit(solution)/shard_map/ppermute | solution.py:17
  188.4 36.5 %collective-permute-start.39 = (bf16[64,1024]{1,0:T(8,128)(2,1)S(1)}, bf16[64,1024]{1,0:T(8,128)(2,1)S(1)}, u32[]{:S(2)}, u32[]{:S(2)}) collective-permute-start(bf16[64,1024]{1,0:T(8,128)(2,1)S(1)} %get-tuple-element.27), channel_id=1, source_target_pairs={{0,1},{1,2},{2,3},{3,0},{4,5},{5,6},{6,7},{7,4},{8,9},{9,10},{10,1... | collective-permute-start | bytes 393224 | tf_op jit(solution)/shard_map/ppermute | solution.py:17
  190.8 18.8 %collective-permute-start.41 = (bf16[64,1024]{1,0:T(8,128)(2,1)S(1)}, bf16[64,1024]{1,0:T(8,128)(2,1)S(1)}, u32[]{:S(2)}, u32[]{:S(2)}) collective-permute-start(bf16[64,1024]{1,0:T(8,128)(2,1)S(1)} %get-tuple-element.26), channel_id=1, source_target_pairs={{0,3},{1,0},{2,1},{3,2},{4,7},{5,4},{6,5},{7,6},{8,11},{9,8},{10,9... | collective-permute-start | bytes 393224 | tf_op jit(solution)/shard_map/ppermute | solution.py:17
  195.7 15.8 %collective-permute-start.37 = (bf16[64,1024]{1,0:T(8,128)(2,1)S(1)}, bf16[64,1024]{1,0:T(8,128)(2,1)S(1)}, u32[]{:S(2)}, u32[]{:S(2)}) collective-permute-start(bf16[64,1024]{1,0:T(8,128)(2,1)S(1)} %get-tuple-element.28), channel_id=1, source_target_pairs={{0,1},{1,2},{2,3},{3,0},{4,5},{5,6},{6,7},{7,4},{8,9},{9,10},{10,1... | collective-permute-start | bytes 393224 | tf_op jit(solution)/shard_map/ppermute | solution.py:17
  200.9 25.9 %collective-permute-start.40 = (bf16[64,1024]{1,0:T(8,128)(2,1)S(1)}, bf16[64,1024]{1,0:T(8,128)(2,1)S(1)}, u32[]{:S(2)}, u32[]{:S(2)}) collective-permute-start(bf16[64,1024]{1,0:T(8,128)(2,1)S(1)} %get-tuple-element.25), channel_id=1, source_target_pairs={{0,3},{1,0},{2,1},{3,2},{4,7},{5,4},{6,5},{7,6},{8,11},{9,8},{10,9... | collective-permute-start | bytes 393224 | tf_op jit(solution)/shard_map/ppermute | solution.py:17
  203.6 30.5 %collective-permute-start.27 = (bf16[64,1024]{1,0:T(8,128)(2,1)S(1)}, bf16[64,1024]{1,0:T(8,128)(2,1)S(1)}, u32[]{:S(2)}, u32[]{:S(2)}) collective-permute-start(bf16[64,1024]{1,0:T(8,128)(2,1)S(1)} %get-tuple-element.21), channel_id=1, source_target_pairs={{0,256},{256,4},{4,260},{260,0},{1,257},{257,5},{5,261},{261,1},{2... | collective-permute-start | bytes 393224 | tf_op jit(solution)/shard_map/ppermute | solution.py:17
  (15 other events, 214.3 us)
